TPU v7x, 32 devices: a whole 2x2x4 slice. The times are simulated.
32 devices in a mesh: group: 2 (over y), sky: 4 (over z), exp: 2 (over x), band: 2 (over core).
Axes of the slice: x: 2, y: 2, z: 4, core: 2. Of those that a mesh axis runs over, the one named last changes fastest.
Arguments:
- sky: bfloat16 [6, 512, 2048], P('band', None, ('group', 'sky')), parts along dimension 2, may hold values from -6 to 6
- observed: bfloat16 [6, 16, 64, 64], P('band', ('group', 'sky', 'exp')), parts along dimension 1, may hold values from -4 to 4
- psf: bfloat16 [6, 16, 625], P('band', ('group', 'sky', 'exp')), parts along dimension 1, may hold values from 0.0039978027 to 0.039794922
- anchor: int32 [6, 16], P('band', 'group'), parts along dimension 1, may hold values from 0 to 2, as said below
- offsets: int32 [6, 2, 16], P('band', None, 'group'), parts along dimension 2, may hold values from 0 to 424
Outputs:
- gradient: float32 [6, 512, 2048], P('band', None, ('group', 'sky')), parts along dimension 2
There are 2 independent parts, one for each index of `group`. A program takes and returns all parts, laid end to end along the dimension named above; each array names one. Nothing has to cross between parts.
Inputs may be any that keep to these rules, and one draw needn't show every extreme that they name: Each exposure's window lies within tile columns a and a + 1 and within the two tile rows. Within each band, the 1 exposures of one device (aligned blocks of 1) have distinct even anchor columns.
All inputs are finite; a program needn't handle non-finite values.
Results may differ from a plain program's by a relative error of at most 0.0028.
Values may be sent and summed in bfloat16 or wider, within the bound.
No kernel may reach another device: no remote copies, remote signals or barrier semaphores. Data moves between devices by JAX's collectives and lax.ppermute only.
A program may use at most 64 MiB of HBM per device.

v0:
```python
import jax
import jax.numpy as jnp
from jax import lax
from jax.sharding import PartitionSpec as P

TILE = 256
PSF = 25
STAMP = 64
TROWS = 2
WIN = 88


def cut_window(block, row_start, col_start):
    return lax.dynamic_slice(block, (row_start, col_start), (WIN, WIN))


def owner_cuts(sky_part, anchor_row, row_off, col_off, owner_index):
    hits = (anchor_row == owner_index) | (anchor_row == owner_index - 1)
    starts = (anchor_row - owner_index) * TILE + col_off + TILE
    present = jnp.any(hits, axis=-1)
    row_sel = jnp.sum(jnp.where(hits, row_off, 0), axis=-1)
    col_sel = jnp.sum(jnp.where(hits, starts, 0), axis=-1)
    padded = jnp.pad(sky_part, ((0, 0), (0, 0), (TILE, TILE)))
    over_bands = jax.vmap(cut_window, in_axes=(0, 0, 0))
    over_peers = jax.vmap(over_bands, in_axes=(None, 1, 1))
    pieces = over_peers(padded, row_sel, col_sel)
    keep_mask = jnp.transpose(present)[:, :, None, None]
    pieces = jnp.where(keep_mask, pieces, jnp.zeros((), pieces.dtype))
    return (pieces, row_sel, col_sel)


def toeplitz(kernel):
    column_gap = (
        jnp.arange(WIN, dtype=jnp.int32)[:, None] - jnp.arange(STAMP, dtype=jnp.int32)[None, :]
    )
    inside = (column_gap >= 0) & (column_gap < PSF)
    tap_index = jnp.clip(column_gap, 0, PSF - 1)
    banded = jnp.take(kernel, tap_index, axis=2)
    return jnp.where(inside, banded, jnp.zeros((), kernel.dtype))


def band_pass(bundle):
    window, kernel, observed_band = bundle
    banded = toeplitz(kernel)
    row_stack = jnp.stack(
        [window[:, shift_row : shift_row + STAMP, :] for shift_row in range(PSF)], axis=1
    )
    model = jnp.einsum("eaic,eacj->eij", row_stack, banded, preferred_element_type=jnp.float32)
    residual = (model - observed_band.astype(jnp.float32)).astype(jnp.bfloat16)
    padded_stack = jnp.stack(
        [
            jnp.pad(residual, ((0, 0), (shift_row, PSF - 1 - shift_row), (0, 0)))
            for shift_row in range(PSF)
        ],
        axis=1,
    )
    backs = jnp.einsum("eayj,eacj->eyc", padded_stack, banded, preferred_element_type=jnp.float32)
    return backs.astype(jnp.bfloat16)


def exposure_work(received, mine_anchor, observed_part, psf_part):
    local_bands, per_device = mine_anchor.shape
    flat_pieces = received.reshape(-1, WIN, WIN)
    band_ids = jnp.arange(local_bands, dtype=jnp.int32)[:, None]
    first_slot = mine_anchor * local_bands + band_ids
    windows = jnp.take(flat_pieces, first_slot, axis=0) + jnp.take(
        flat_pieces, first_slot + local_bands, axis=0
    )
    kernels = psf_part.reshape(local_bands, per_device, PSF, PSF)
    backs = lax.map(band_pass, (windows, kernels, observed_part))
    owner_ids = jnp.arange(received.shape[0], dtype=jnp.int32)[None, :, None]
    chosen_anchor = mine_anchor[:, None, :]
    routing = ((chosen_anchor == owner_ids) | (chosen_anchor == owner_ids - 1)).astype(jnp.bfloat16)
    slots = jnp.einsum("bte,bexy->tbxy", routing, backs, preferred_element_type=jnp.float32)
    return slots.astype(jnp.bfloat16)


def add_window(block, update, row_start, col_start):
    current = lax.dynamic_slice(block, (row_start, col_start), (WIN, WIN))
    return lax.dynamic_update_slice(
        block, current + update.astype(jnp.float32), (row_start, col_start)
    )


def owner_adds(returned, row_sel, col_sel):
    local_bands = returned.shape[1]
    start = jnp.zeros((local_bands, TROWS * TILE, 3 * TILE), jnp.float32)

    def visit(peer_pos, total):
        update = lax.dynamic_index_in_dim(returned, peer_pos, 0, keepdims=False)
        row_pick = lax.dynamic_index_in_dim(row_sel, peer_pos, 1, keepdims=False)
        col_pick = lax.dynamic_index_in_dim(col_sel, peer_pos, 1, keepdims=False)
        return jax.vmap(add_window)(total, update, row_pick, col_pick)

    total = lax.fori_loop(0, returned.shape[0], visit, start)
    return total[:, :, TILE : 2 * TILE]


def on_device(sky, observed, psf, anchor, offsets):
    local_bands = sky.shape[0]
    per_device = observed.shape[1]
    sky_count = lax.axis_size("sky")
    exp_count = lax.axis_size("exp")
    owner_index = lax.axis_index("sky")
    replica_index = lax.axis_index("exp")
    anchor_all = anchor.reshape(local_bands, sky_count, exp_count, per_device)
    anchor_row = lax.dynamic_index_in_dim(anchor_all, replica_index, 2, keepdims=False)
    offset_all = offsets.reshape(local_bands, 2, sky_count, exp_count, per_device)
    offset_row = lax.dynamic_index_in_dim(offset_all, replica_index, 3, keepdims=False)
    mine_anchor = lax.dynamic_index_in_dim(anchor_row, owner_index, 1, keepdims=False)
    row_off = offset_row[:, 0]
    col_off = offset_row[:, 1]
    pieces, row_sel, col_sel = owner_cuts(sky, anchor_row, row_off, col_off, owner_index)
    received = lax.all_to_all(pieces, "sky", split_axis=0, concat_axis=0, tiled=True)
    slots = exposure_work(received, mine_anchor, observed, psf)
    returned = lax.all_to_all(slots, "sky", split_axis=0, concat_axis=0, tiled=True)
    gradient = owner_adds(returned, row_sel, col_sel)
    return lax.psum(gradient, "exp")


def solution(mesh):
    return jax.shard_map(
        on_device,
        mesh=mesh,
        in_specs=(
            P("band", None, ("group", "sky")),
            P("band", ("group", "sky", "exp"), None, None),
            P("band", ("group", "sky", "exp"), None),
            P("band", "group"),
            P("band", None, "group"),
        ),
        out_specs=P("band", None, ("group", "sky")),
        check_vma=False,
    )
```

profile of v0, /device:TPU:0, one launch (start us, length us, event | category | flops | bytes accessed | tf_op | source)
XLA Modules:
  0.0 369.1 jit_solution(10511360675664639365)
XLA Ops:
  10.2 32.6 %while.34 = (s32[]{:T(128)}, bf16[3,512,768]{2,1,0:T(8,128)(2,1)S(1)}, s32[12,3]{0,1:T(4,128)S(1)}, bf16[12,88,88]{2,1,0:T(8,128)(2,1)S(1)}, s32[]{:T(128)}) while((s32[]{:T(128)}, bf16[3,512,768]{2,1,0:T(8,128)(2,1)S(1)}, s32[12,3]{0,1:T(4,128)S(1)}, bf16[12,88,88]{2,1,0:T(8,128)(2,1)S(1)}, s32[]{:T(128)}) %tuple.128), condition=%wide.while_cond.1, body=%wide.while_body.1.sunk | while | flops 2 | bytes 45193 | solution.py:14
  43.6 6.3 %all-to-all-start = ((bf16[4,3,88,88]{3,2,1,0:T(8,128)(2,1)}), bf16[4,3,88,88]{3,2,1,0:T(8,128)(2,1)S(1)}, u32[]{:S(2)}, u32[]{:S(2)}) async-start(bf16[4,3,88,88]{3,2,1,0:T(8,128)(2,1)} %broadcast_select_fusion), calls=%async_computation | async-start | bytes 540672 | tf_op jit(solution)/shard_map/all_to_all | solution.py:114
  50.2 8.8 %all-to-all-done = bf16[4,3,88,88]{3,2,1,0:T(8,128)(2,1)S(1)} async-done(((bf16[4,3,88,88]{3,2,1,0:T(8,128)(2,1)}), bf16[4,3,88,88]{3,2,1,0:T(8,128)(2,1)S(1)}, u32[]{:S(2)}, u32[]{:S(2)}) %all-to-all-start) | async-done | bytes 185888 | tf_op jit(solution)/shard_map/all_to_all | solution.py:114
  60.2 50.5 %while.30 = (s32[]{:T(128)}, bf16[3,1,88,88]{3,2,1,0:T(8,128)(2,1)S(1)}, bf16[3,1,88,88]{3,2,1,0:T(8,128)(2,1)S(1)}, bf16[3,1,25,25]{3,2,0,1:T(8,128)(2,1)S(1)}, bf16[3,1,64,64]{3,2,1,0:T(8,128)(2,1)}, /*index=5*/s32[]{:T(128)}) while((s32[]{:T(128)}, bf16[3,1,88,88]{3,2,1,0:T(8,128)(2,1)S(1)}, bf16[3,1,88,88]{3,2,1,0:T(8,128)(2,1)S(1)}, ...), condition=%wide.region_1.3_spmd, body=%wide.region_0.2_spmd.sunk | while | flops 43482688 | bytes 4417765 | solution.py:70
  61.8 10.7 %gather_fusion = bf16[5632,25]{1,0:T(8,128)(2,1)S(1)} fusion(bf16[25,25]{0,1:T(8,128)(2,1)S(1)} %bitcast.439, s32[6144]{0:T(1024)S(1)} %pad_clamp_fusion.4), kind=kCustom, calls=%fused_computation.1.clone.1 | custom fusion | bytes 585728 | tf_op jit(solution)/shard_map/while/body/eval_jaxpr/jit(_take)/gather | solution.py:38
  78.6 10.7 %gather_fusion = bf16[5632,25]{1,0:T(8,128)(2,1)S(1)} fusion(bf16[25,25]{0,1:T(8,128)(2,1)S(1)} %bitcast.439, s32[6144]{0:T(1024)S(1)} %pad_clamp_fusion.4), kind=kCustom, calls=%fused_computation.1.clone.1 | custom fusion | bytes 585728 | tf_op jit(solution)/shard_map/while/body/eval_jaxpr/jit(_take)/gather | solution.py:38
  95.5 10.7 %gather_fusion = bf16[5632,25]{1,0:T(8,128)(2,1)S(1)} fusion(bf16[25,25]{0,1:T(8,128)(2,1)S(1)} %bitcast.439, s32[6144]{0:T(1024)S(1)} %pad_clamp_fusion.4), kind=kCustom, calls=%fused_computation.1.clone.1 | custom fusion | bytes 585728 | tf_op jit(solution)/shard_map/while/body/eval_jaxpr/jit(_take)/gather | solution.py:38
  111.6 3.4 all-to-all-start.1
  115.1 7.0 %all-to-all-done.1 = bf16[4,3,88,88]{3,2,1,0:T(8,128)(2,1)S(1)} async-done(((bf16[4,3,88,88]{3,2,1,0:T(8,128)(2,1)}), bf16[4,3,88,88]{3,2,1,0:T(8,128)(2,1)S(1)}, u32[]{:S(2)}, u32[]{:S(2)}) %all-to-all-start.1) | async-done | bytes 185888 | tf_op jit(solution)/shard_map/all_to_all | solution.py:116
  124.6 180.9 %while.33 = (s32[]{:T(128)}, f32[3,512,768]{2,1,0:T(8,128)}, s32[3,4]{1,0:T(4,128)S(1)}, s32[3,4]{1,0:T(4,128)S(1)}, bf16[4,3,88,88]{3,2,1,0:T(8,128)(2,1)S(1)},...) while((s32[]{:T(128)}, f32[3,512,768]{2,1,0:T(8,128)}, ...), condition=%wide.region_4.6_spmd, body=%wide.region_2.5_spmd.sunk | while | flops 54288 | bytes 464029 | solution.py:95
  124.8 10.6 %while.35 = (s32[]{:T(128)}, f32[3,512,768]{2,1,0:T(8,128)}, s32[3,3]{1,0:T(4,128)S(1)}, f32[3,88,88]{2,1,0:T(8,128)S(1)}, s32[]{:T(128)}) while((s32[]{:T(128)}, f32[3,512,768]{2,1,0:T(8,128)}, s32[3,3]{1,0:T(4,128)S(1)}, f32[3,88,88]{2,1,0:T(8,128)S(1)}, s32[]{:T(128)}) %tuple.122), condition=%wide.while_cond, body=%wide.while_body.sunk | while | flops 2 | bytes 76169 | solution.py:79
  125.5 2.9 dynamic-slice_dynamic-update-slice_fusion.5
  129.0 2.9 dynamic-slice_dynamic-update-slice_fusion.5
  132.5 2.9 dynamic-slice_dynamic-update-slice_fusion.5
  135.4 34.3 %while.36 = (s32[]{:T(128)}, f32[3,512,768]{2,1,0:T(8,128)}, s32[3,3]{1,0:T(4,128)S(1)}, f32[3,88,88]{2,1,0:T(8,128)S(1)}, s32[]{:T(128)}, /*index=5*/s32[3]{0:T(128)S(1)}) while((s32[]{:T(128)}, f32[3,512,768]{2,1,0:T(8,128)}, s32[3,3]{1,0:T(4,128)S(1)}, f32[3,88,88]{2,1,0:T(8,128)S(1)}, s32[]{:T(128)}, /*index=5*/s32[3]{0:T(128)S(1)}) %tuple.139), condition=%wide.while_cond.2, body=%wide.while_body.2.sunk | while | flops 7763 | bytes 155055 | solution.py:80
  136.1 2.6 and_reduce_fusion.2
  138.7 3.4 dynamic-slice_select_fusion.2
  142.1 4.9 %dynamic-update-slice.212 = f32[3,512,768]{2,1,0:T(8,128)} dynamic-update-slice(f32[3,512,768]{2,1,0:T(8,128)} %get-tuple-element.491, f32[1,88,88]{2,1,0:T(8,128)S(1)} %dynamic-slice_select_fusion.2, s32[]{:T(128)} %bitcast.433, s32[]{:T(128)} %bitcast.434, s32[]{:T(128)} %bitcast.435) | dynamic-update-slice | bytes 61956 | tf_op jit(solution)/shard_map/while/body/eval_jaxpr/vmap(vmap())/scatter
  147.7 2.6 and_reduce_fusion.2
  150.2 3.4 dynamic-slice_select_fusion.2
  153.7 4.7 %dynamic-update-slice.212 = f32[3,512,768]{2,1,0:T(8,128)} dynamic-update-slice(f32[3,512,768]{2,1,0:T(8,128)} %get-tuple-element.491, f32[1,88,88]{2,1,0:T(8,128)S(1)} %dynamic-slice_select_fusion.2, s32[]{:T(128)} %bitcast.433, s32[]{:T(128)} %bitcast.434, s32[]{:T(128)} %bitcast.435) | dynamic-update-slice | bytes 61956 | tf_op jit(solution)/shard_map/while/body/eval_jaxpr/vmap(vmap())/scatter
  159.0 2.6 and_reduce_fusion.2
  161.6 3.4 dynamic-slice_select_fusion.2
  165.0 4.7 %dynamic-update-slice.212 = f32[3,512,768]{2,1,0:T(8,128)} dynamic-update-slice(f32[3,512,768]{2,1,0:T(8,128)} %get-tuple-element.491, f32[1,88,88]{2,1,0:T(8,128)S(1)} %dynamic-slice_select_fusion.2, s32[]{:T(128)} %bitcast.433, s32[]{:T(128)} %bitcast.434, s32[]{:T(128)} %bitcast.435) | dynamic-update-slice | bytes 61956 | tf_op jit(solution)/shard_map/while/body/eval_jaxpr/vmap(vmap())/scatter
  170.0 10.6 %while.35 = (s32[]{:T(128)}, f32[3,512,768]{2,1,0:T(8,128)}, s32[3,3]{1,0:T(4,128)S(1)}, f32[3,88,88]{2,1,0:T(8,128)S(1)}, s32[]{:T(128)}) while((s32[]{:T(128)}, f32[3,512,768]{2,1,0:T(8,128)}, s32[3,3]{1,0:T(4,128)S(1)}, f32[3,88,88]{2,1,0:T(8,128)S(1)}, s32[]{:T(128)}) %tuple.122), condition=%wide.while_cond, body=%wide.while_body.sunk | while | flops 2 | bytes 76169 | solution.py:79
  170.7 2.9 dynamic-slice_dynamic-update-slice_fusion.5
  174.2 2.9 dynamic-slice_dynamic-update-slice_fusion.5
  177.7 2.9 dynamic-slice_dynamic-update-slice_fusion.5
  180.6 34.3 %while.36 = (s32[]{:T(128)}, f32[3,512,768]{2,1,0:T(8,128)}, s32[3,3]{1,0:T(4,128)S(1)}, f32[3,88,88]{2,1,0:T(8,128)S(1)}, s32[]{:T(128)}, /*index=5*/s32[3]{0:T(128)S(1)}) while((s32[]{:T(128)}, f32[3,512,768]{2,1,0:T(8,128)}, s32[3,3]{1,0:T(4,128)S(1)}, f32[3,88,88]{2,1,0:T(8,128)S(1)}, s32[]{:T(128)}, /*index=5*/s32[3]{0:T(128)S(1)}) %tuple.139), condition=%wide.while_cond.2, body=%wide.while_body.2.sunk | while | flops 7763 | bytes 155055 | solution.py:80
  181.3 2.6 and_reduce_fusion.2
  183.9 3.4 dynamic-slice_select_fusion.2
  187.3 4.7 %dynamic-update-slice.212 = f32[3,512,768]{2,1,0:T(8,128)} dynamic-update-slice(f32[3,512,768]{2,1,0:T(8,128)} %get-tuple-element.491, f32[1,88,88]{2,1,0:T(8,128)S(1)} %dynamic-slice_select_fusion.2, s32[]{:T(128)} %bitcast.433, s32[]{:T(128)} %bitcast.434, s32[]{:T(128)} %bitcast.435) | dynamic-update-slice | bytes 61956 | tf_op jit(solution)/shard_map/while/body/eval_jaxpr/vmap(vmap())/scatter
  192.7 2.6 and_reduce_fusion.2
  195.3 3.4 dynamic-slice_select_fusion.2
  198.7 4.7 %dynamic-update-slice.212 = f32[3,512,768]{2,1,0:T(8,128)} dynamic-update-slice(f32[3,512,768]{2,1,0:T(8,128)} %get-tuple-element.491, f32[1,88,88]{2,1,0:T(8,128)S(1)} %dynamic-slice_select_fusion.2, s32[]{:T(128)} %bitcast.433, s32[]{:T(128)} %bitcast.434, s32[]{:T(128)} %bitcast.435) | dynamic-update-slice | bytes 61956 | tf_op jit(solution)/shard_map/while/body/eval_jaxpr/vmap(vmap())/scatter
  204.0 2.6 and_reduce_fusion.2
  206.6 3.4 dynamic-slice_select_fusion.2
  210.0 4.9 %dynamic-update-slice.212 = f32[3,512,768]{2,1,0:T(8,128)} dynamic-update-slice(f32[3,512,768]{2,1,0:T(8,128)} %get-tuple-element.491, f32[1,88,88]{2,1,0:T(8,128)S(1)} %dynamic-slice_select_fusion.2, s32[]{:T(128)} %bitcast.433, s32[]{:T(128)} %bitcast.434, s32[]{:T(128)} %bitcast.435) | dynamic-update-slice | bytes 61956 | tf_op jit(solution)/shard_map/while/body/eval_jaxpr/vmap(vmap())/scatter
  215.1 10.6 %while.35 = (s32[]{:T(128)}, f32[3,512,768]{2,1,0:T(8,128)}, s32[3,3]{1,0:T(4,128)S(1)}, f32[3,88,88]{2,1,0:T(8,128)S(1)}, s32[]{:T(128)}) while((s32[]{:T(128)}, f32[3,512,768]{2,1,0:T(8,128)}, s32[3,3]{1,0:T(4,128)S(1)}, f32[3,88,88]{2,1,0:T(8,128)S(1)}, s32[]{:T(128)}) %tuple.122), condition=%wide.while_cond, body=%wide.while_body.sunk | while | flops 2 | bytes 76169 | solution.py:79
  215.8 2.9 dynamic-slice_dynamic-update-slice_fusion.5
  219.4 2.9 dynamic-slice_dynamic-update-slice_fusion.5
  222.9 2.9 dynamic-slice_dynamic-update-slice_fusion.5
  225.8 34.5 %while.36 = (s32[]{:T(128)}, f32[3,512,768]{2,1,0:T(8,128)}, s32[3,3]{1,0:T(4,128)S(1)}, f32[3,88,88]{2,1,0:T(8,128)S(1)}, s32[]{:T(128)}, /*index=5*/s32[3]{0:T(128)S(1)}) while((s32[]{:T(128)}, f32[3,512,768]{2,1,0:T(8,128)}, s32[3,3]{1,0:T(4,128)S(1)}, f32[3,88,88]{2,1,0:T(8,128)S(1)}, s32[]{:T(128)}, /*index=5*/s32[3]{0:T(128)S(1)}) %tuple.139), condition=%wide.while_cond.2, body=%wide.while_body.2.sunk | while | flops 7763 | bytes 155055 | solution.py:80
  229.0 3.4 dynamic-slice_select_fusion.2
  232.5 4.8 %dynamic-update-slice.212 = f32[3,512,768]{2,1,0:T(8,128)} dynamic-update-slice(f32[3,512,768]{2,1,0:T(8,128)} %get-tuple-element.491, f32[1,88,88]{2,1,0:T(8,128)S(1)} %dynamic-slice_select_fusion.2, s32[]{:T(128)} %bitcast.433, s32[]{:T(128)} %bitcast.434, s32[]{:T(128)} %bitcast.435) | dynamic-update-slice | bytes 61956 | tf_op jit(solution)/shard_map/while/body/eval_jaxpr/vmap(vmap())/scatter
  240.5 3.4 dynamic-slice_select_fusion.2
  243.9 4.9 %dynamic-update-slice.212 = f32[3,512,768]{2,1,0:T(8,128)} dynamic-update-slice(f32[3,512,768]{2,1,0:T(8,128)} %get-tuple-element.491, f32[1,88,88]{2,1,0:T(8,128)S(1)} %dynamic-slice_select_fusion.2, s32[]{:T(128)} %bitcast.433, s32[]{:T(128)} %bitcast.434, s32[]{:T(128)} %bitcast.435) | dynamic-update-slice | bytes 61956 | tf_op jit(solution)/shard_map/while/body/eval_jaxpr/vmap(vmap())/scatter
  249.5 2.6 and_reduce_fusion.2
  252.0 3.4 dynamic-slice_select_fusion.2
  255.5 4.9 %dynamic-update-slice.212 = f32[3,512,768]{2,1,0:T(8,128)} dynamic-update-slice(f32[3,512,768]{2,1,0:T(8,128)} %get-tuple-element.491, f32[1,88,88]{2,1,0:T(8,128)S(1)} %dynamic-slice_select_fusion.2, s32[]{:T(128)} %bitcast.433, s32[]{:T(128)} %bitcast.434, s32[]{:T(128)} %bitcast.435) | dynamic-update-slice | bytes 61956 | tf_op jit(solution)/shard_map/while/body/eval_jaxpr/vmap(vmap())/scatter
  260.6 10.6 %while.35 = (s32[]{:T(128)}, f32[3,512,768]{2,1,0:T(8,128)}, s32[3,3]{1,0:T(4,128)S(1)}, f32[3,88,88]{2,1,0:T(8,128)S(1)}, s32[]{:T(128)}) while((s32[]{:T(128)}, f32[3,512,768]{2,1,0:T(8,128)}, s32[3,3]{1,0:T(4,128)S(1)}, f32[3,88,88]{2,1,0:T(8,128)S(1)}, s32[]{:T(128)}) %tuple.122), condition=%wide.while_cond, body=%wide.while_body.sunk | while | flops 2 | bytes 76169 | solution.py:79
  261.2 2.9 dynamic-slice_dynamic-update-slice_fusion.5
  264.8 2.9 dynamic-slice_dynamic-update-slice_fusion.5
  268.3 2.9 dynamic-slice_dynamic-update-slice_fusion.5
  271.2 34.3 %while.36 = (s32[]{:T(128)}, f32[3,512,768]{2,1,0:T(8,128)}, s32[3,3]{1,0:T(4,128)S(1)}, f32[3,88,88]{2,1,0:T(8,128)S(1)}, s32[]{:T(128)}, /*index=5*/s32[3]{0:T(128)S(1)}) while((s32[]{:T(128)}, f32[3,512,768]{2,1,0:T(8,128)}, s32[3,3]{1,0:T(4,128)S(1)}, f32[3,88,88]{2,1,0:T(8,128)S(1)}, s32[]{:T(128)}, /*index=5*/s32[3]{0:T(128)S(1)}) %tuple.139), condition=%wide.while_cond.2, body=%wide.while_body.2.sunk | while | flops 7763 | bytes 155055 | solution.py:80
  274.5 3.4 dynamic-slice_select_fusion.2
  277.9 4.9 %dynamic-update-slice.212 = f32[3,512,768]{2,1,0:T(8,128)} dynamic-update-slice(f32[3,512,768]{2,1,0:T(8,128)} %get-tuple-element.491, f32[1,88,88]{2,1,0:T(8,128)S(1)} %dynamic-slice_select_fusion.2, s32[]{:T(128)} %bitcast.433, s32[]{:T(128)} %bitcast.434, s32[]{:T(128)} %bitcast.435) | dynamic-update-slice | bytes 61956 | tf_op jit(solution)/shard_map/while/body/eval_jaxpr/vmap(vmap())/scatter
  286.0 3.4 dynamic-slice_select_fusion.2
  289.4 4.7 %dynamic-update-slice.212 = f32[3,512,768]{2,1,0:T(8,128)} dynamic-update-slice(f32[3,512,768]{2,1,0:T(8,128)} %get-tuple-element.491, f32[1,88,88]{2,1,0:T(8,128)S(1)} %dynamic-slice_select_fusion.2, s32[]{:T(128)} %bitcast.433, s32[]{:T(128)} %bitcast.434, s32[]{:T(128)} %bitcast.435) | dynamic-update-slice | bytes 61956 | tf_op jit(solution)/shard_map/while/body/eval_jaxpr/vmap(vmap())/scatter
  297.4 3.4 dynamic-slice_select_fusion.2
  300.8 4.7 %dynamic-update-slice.212 = f32[3,512,768]{2,1,0:T(8,128)} dynamic-update-slice(f32[3,512,768]{2,1,0:T(8,128)} %get-tuple-element.491, f32[1,88,88]{2,1,0:T(8,128)S(1)} %dynamic-slice_select_fusion.2, s32[]{:T(128)} %bitcast.433, s32[]{:T(128)} %bitcast.434, s32[]{:T(128)} %bitcast.435) | dynamic-update-slice | bytes 61956 | tf_op jit(solution)/shard_map/while/body/eval_jaxpr/vmap(vmap())/scatter
  305.5 2.7 slice.161
  308.2 51.4 %all-reduce.28.cloned.1.call-done = f32[3,512,256]{2,1,0:T(8,128)} async-done(((f32[3,512,256]{2,1,0:T(8,128)}), f32[3,512,256]{2,1,0:T(8,128)}) %all-reduce.28.cloned.1.call-update) | async-done | bytes 1572880 | tf_op jit(solution)/shard_map/psum | solution.py:118
  359.6 2.7 copy.146
  (341 shorter events, 89.5 us)
Async XLA Ops:
  6.5 43.5 %copy-start.2 = (bf16[3,1,625]{2,0,1:T(4,128)(2,1)S(1)}, bf16[3,1,625]{2,0,1:T(4,128)(2,1)}, u32[]{:S(2)}) copy-start(bf16[3,1,625]{2,0,1:T(4,128)(2,1)} %param.13) | copy-start | bytes 11254
  43.6 15.4 %all-to-all-start = ((bf16[4,3,88,88]{3,2,1,0:T(8,128)(2,1)}), bf16[4,3,88,88]{3,2,1,0:T(8,128)(2,1)S(1)}, u32[]{:S(2)}, u32[]{:S(2)}) async-start(bf16[4,3,88,88]{3,2,1,0:T(8,128)(2,1)} %broadcast_select_fusion), calls=%async_computation | async-start | bytes 540672 | tf_op jit(solution)/shard_map/all_to_all | solution.py:114
  110.7 13.9 %copy-start = (s32[3]{0:T(128)S(1)}, s32[3]{0:T(128)}, u32[]{:S(2)}) copy-start(s32[3]{0:T(128)} %constant.628) | copy-start | bytes 40
  110.7 13.8 %copy-start.1 = (s32[2]{0:T(128)S(1)}, s32[2]{0:T(128)}, u32[]{:S(2)}) copy-start(s32[2]{0:T(128)} %constant.168.clone.1) | copy-start | bytes 28
  111.6 10.5 %all-to-all-start.1 = ((bf16[4,3,88,88]{3,2,1,0:T(8,128)(2,1)}), bf16[4,3,88,88]{3,2,1,0:T(8,128)(2,1)S(1)}, u32[]{:S(2)}, u32[]{:S(2)}) async-start(bf16[4,3,88,88]{3,2,1,0:T(8,128)(2,1)} %fusion.26), calls=%async_computation.1 | async-start | bytes 540672 | tf_op jit(solution)/shard_map/all_to_all | solution.py:116
  115.0 244.5 %all-reduce.28.cloned.1.call-start = ((), (), s32[]{:S(2)}) async-start(), calls=%async_computation.2 | async-start | bytes 3145728 | tf_op jit(solution)/shard_map/psum | solution.py:118
Sparse Core Ops, SparseCore 0:
  308.3 51.2 all-reduce.27
where the time goes:
time: 374 us; the launch traced here: 369 us
  local copies, waits for them, and re-layouts  201 us (54%)
  other arithmetic  75 us (20%)
  waiting for transfers between devices  67.2 us (18%)
  between operations  13.5 us (4%)
  starting transfers between devices  9.84 us (3%)
    gather x72, local copies, waits for them, and re-layouts  74.7 us
    scatter x24, other arithmetic  71.9 us
    scatter x36, local copies, waits for them, and re-layouts  65.4 us
    psum x1, waiting for transfers between devices, on_device(): return lax.psum(gradient, 'exp')  51.4 us
    gather x6, local copies, waits for them, and re-layouts, toeplitz(): banded = jnp.take(kernel, tap_index, axis=2)  37.8 us
    all_to_all x1, waiting for transfers between devices, on_device(): lax.all_to_all(pieces, 'sky', split_axis=0, concat_axis=0, tiled=True)  8.8 us
  transfers between devices with their start and end apart: 3, of which 3 were waited for; matrix products, arithmetic and copies ran while one was open for 0% of the time, Pallas kernels for 0%

commit v1 on v0

v1 whole, which is shorter than its diff:
```python
import functools

import jax
import jax.numpy as jnp
import numpy as np
from jax import lax
from jax.experimental import pallas as pl
from jax.experimental.pallas import tpu as pltpu
from jax.sharding import PartitionSpec as P

TILE = 256
PSF = 25
STAMP = 64
HALF = STAMP // 2
WIN = 88
LANES = 128
PAIRS = (PSF + 1) // 2
ROWS = 48
WPAD = 96
OWN = TILE // LANES
STRIP = OWN + 1
EDGE = PSF - 1
FOLD = 4
TOGETHER = 2


def lane_of(shape):
    return lax.broadcasted_iota(jnp.int32, shape, 1)


def row_of(shape):
    return lax.broadcasted_iota(jnp.int32, shape, 0)


def spread_table():
    k = np.arange(PSF * PSF) % (2 * PSF)
    place = np.where(k < PSF, -k % LANES, STAMP - (k - PSF))
    return jnp.asarray(place[:, None] == np.arange(LANES)[None, :], jnp.bfloat16)


def prep_kernel(sky_hbm, table_hbm, obs_hbm, psf_hbm, blocks_ref, border_ref, edge, table, obs, psf, sems):
    bands, per_device = obs.shape[:2]
    parity = lax.axis_index("sky") % 2
    side = pl.multiple_of((1 - parity) * (TILE - LANES), LANES)
    copies = [
        pltpu.make_async_copy(src, dst, sems.at[at])
        for at, (src, dst) in enumerate(
            [(psf_hbm, psf), (table_hbm, table), (obs_hbm, obs), (sky_hbm.at[:, :, pl.ds(side, LANES)], edge)]
        )
    ]
    for copy in copies:
        copy.start()
    for copy in copies[:3]:
        copy.wait()
    taps = PSF * PSF
    gap = lane_of((16, taps)) - 2 * PSF * row_of((16, taps))
    inside = (gap >= 0) & (gap < 2 * PSF)
    for b in range(bands):
        for x in range(per_device):
            stamp = obs[b, x].astype(jnp.float32)
            both = jnp.concatenate([stamp[:HALF], stamp[HALF:]], axis=1)
            blocks_ref[x, b, 0:HALF, :] = both.astype(jnp.bfloat16)
            flat = jnp.broadcast_to(psf[b, x : x + 1, :].astype(jnp.float32), (16, taps))
            mine = jnp.where(inside, flat, 0.0).astype(jnp.bfloat16)
            rows = jnp.dot(mine, table[...], preferred_element_type=jnp.float32)
            blocks_ref[x, b, HALF:ROWS, :] = rows.astype(jnp.bfloat16)
    copies[3].wait()
    fold = edge.shape[1] // FOLD
    lane = lane_of((fold, LANES))
    base = (1 - parity) * WIN
    for b in range(bands):
        turned = []
        for g in range(FOLD):
            part = edge[b, g * fold : (g + 1) * fold, :].astype(jnp.float32)
            turned.append(pltpu.roll(part, (base + WIN * g) % LANES, 1))
        for t in range(STRIP):
            limit = WIN * (t + 1) - LANES * t
            tile = jnp.where(lane < limit, turned[t], turned[t + 1])
            border_ref[b, :, t * LANES : (t + 1) * LANES] = tile.astype(jnp.bfloat16)


def prep(sky, observed, psf):
    bands, per_device = observed.shape[:2]
    rows_total = sky.shape[1]
    table = spread_table()
    anywhere = pl.BlockSpec(memory_space=pl.ANY)
    vmem = pl.BlockSpec(memory_space=pltpu.VMEM)
    return pl.pallas_call(
        prep_kernel,
        out_shape=(
            jax.ShapeDtypeStruct((per_device, bands, ROWS, LANES), jnp.bfloat16),
            jax.ShapeDtypeStruct((bands, rows_total // FOLD, STRIP * LANES), jnp.bfloat16),
        ),
        in_specs=[anywhere] * 4,
        out_specs=(vmem, vmem),
        scratch_shapes=[
            pltpu.VMEM((bands, rows_total, LANES), jnp.bfloat16),
            pltpu.VMEM(table.shape, jnp.bfloat16),
            pltpu.VMEM(observed.shape, jnp.bfloat16),
            pltpu.VMEM(psf.shape, jnp.bfloat16),
            pltpu.SemaphoreType.DMA((4,)),
        ],
        name="prep",
    )(sky, table, observed, psf)


def list_jobs(jobs, anchor_ref, offset_ref, column, bands, slots, per_device):
    parity = column % 2
    low = jnp.where(parity == 0, -1, TILE - WIN)
    high = jnp.where(parity == 0, TILE, 2 * TILE)
    count = jnp.int32(0)

    def visit(b, n, count):
        for x in range(per_device):
            i = n * per_device + x
            left = offset_ref[b, 1, i]
            meets = (anchor_ref[b, i] == column - parity) & (left > low) & (left < high)
            jobs[0, count] = jnp.int32(b)
            jobs[1, count] = jnp.int32(n)
            jobs[2, count] = offset_ref[b, 0, i]
            jobs[3, count] = left - parity * (TILE - LANES)
            count = count + meets.astype(jnp.int32)
        return count

    for b in range(bands):
        if slots <= 8:
            for n in range(slots):
                count = visit(b, n, count)
        else:
            count = lax.fori_loop(0, slots, functools.partial(visit, b), count)
    for extra in range(TOGETHER - 1):
        for field in range(4):
            jobs[field, count + extra] = jnp.int32(0)
    return count


def work_kernel(layout, slots, per_device, anchor_ref, offset_ref, sky_hbm, halo_hbm, *rest):
    pieces = rest[: len(layout)]
    rest = rest[len(layout) :]
    out_hbm, jobs, strip, total, halo, blocks, cut, banded, wide, rows_a, rows_r, sems, out_sems = rest
    bands, rows_total = sky_hbm.shape[:2]
    column = lax.axis_index("sky")
    parity = column % 2
    position = column * lax.axis_size("exp") + lax.axis_index("exp")

    copies = [pltpu.make_async_copy(halo_hbm, halo, sems.at[0])]
    for t in range(OWN):
        copies.append(
            pltpu.make_async_copy(
                sky_hbm.at[:, :, pl.ds(t * LANES, LANES)],
                strip.at[:, parity + t, pl.ds(0, rows_total), :],
                sems.at[1 + t],
            )
        )
    at = 1 + OWN
    for masks, piece in zip(layout, pieces):
        if masks is None:
            copies.append(pltpu.make_async_copy(piece, blocks, sems.at[at]))
            at += 1
        else:
            for j, mask in enumerate(masks):
                dst = blocks.at[jnp.bitwise_xor(position, mask)]
                copies.append(pltpu.make_async_copy(piece.at[j], dst, sems.at[at]))
                at += 1
    for copy in copies:
        copy.start()

    count = list_jobs(jobs, anchor_ref, offset_ref, column, bands, slots, per_device)
    rows_r[...] = jnp.zeros(rows_r.shape, jnp.float32)
    for b in range(bands):
        for t in range(OWN):
            total[b, parity + t] = jnp.zeros((rows_total, LANES), jnp.float32)
        for t in range(STRIP):
            strip[b, t, rows_total : rows_total + 16, :] = jnp.zeros((16, LANES), jnp.bfloat16)

    copies[0].wait()
    fold = rows_total // FOLD
    place = parity * (LANES - WIN)
    lane = jnp.bitwise_and(lane_of((fold, LANES)) - place, LANES - 1)
    for b in range(bands):
        tiles = [halo[b, :, t * LANES : (t + 1) * LANES].astype(jnp.float32) for t in range(STRIP)]
        for g in range(FOLD):
            shift = (place + LANES - WIN * g % LANES) % LANES
            first = WIN * g // LANES
            limit = LANES * (first + 1) - WIN * g
            value = pltpu.roll(tiles[first], shift, 1)
            if limit < WIN:
                value = jnp.where(lane < limit, value, pltpu.roll(tiles[first + 1], shift, 1))
            strip[b, OWN * (1 - parity), g * fold : (g + 1) * fold, :] = value.astype(jnp.bfloat16)
    for copy in copies[1:]:
        copy.wait()

    lane_w = lane_of((WPAD, LANES))
    gap = row_of((WPAD, LANES)) - lane_w % STAMP
    inside = (gap >= 0) & (gap < PSF) & (row_of((WPAD, LANES)) < WIN)
    lane_c = lane_of((WPAD + 16, LANES))
    lane_b = lane_of((WIN, LANES))
    low = lane_of((STAMP, LANES)) < STAMP

    def one(job, u):
        b, n, top, start = (jobs[field, job] for field in range(4))
        tile = lax.shift_right_logical(start, 7)
        shift = jnp.bitwise_and(start, LANES - 1)
        after = jnp.minimum(tile + 1, STRIP - 1)
        back_shift = jnp.bitwise_and(LANES - shift, LANES - 1)
        base = pl.multiple_of(jnp.bitwise_and(top, -16), 16)
        left = pltpu.roll(strip[b, tile, pl.ds(base, WPAD + 16), :].astype(jnp.float32), back_shift, 1)
        right = pltpu.roll(strip[b, after, pl.ds(base, WPAD + 16), :].astype(jnp.float32), back_shift, 1)
        cut[u] = jnp.where(lane_c < LANES - shift, left, right)
        window = cut[u, pl.ds(top - base, WPAD), :].astype(jnp.bfloat16)
        taps = blocks[n, b, HALF:ROWS, :].astype(jnp.float32)
        for m in range(PAIRS):
            spread = jnp.broadcast_to(taps[m : m + 1, :], (WPAD, LANES))
            turned = pltpu.roll(spread, 0, 1, stride=1, stride_axis=0)
            banded[u, :, m * LANES : (m + 1) * LANES] = jnp.where(inside, turned, 0.0).astype(jnp.bfloat16)
        product = jnp.dot(window[:, :WPAD], banded[u], preferred_element_type=jnp.float32)
        for m in range(PAIRS):
            wide[u, m] = product[:, m * LANES : (m + 1) * LANES]
        acc = wide[u, 0, 0:72, :]
        for m in range(1, PAIRS):
            acc = acc + wide[u, m, 2 * m : 2 * m + 72, :]
        rows_a[u] = acc
        model = rows_a[u, 0:STAMP, :] + pltpu.roll(rows_a[u, 1 : STAMP + 1, :], STAMP, 1)
        obs = blocks[n, b, 0:HALF, :].astype(jnp.float32)
        obs = jnp.concatenate([obs, pltpu.roll(obs, STAMP, 1)], axis=0)
        residual = (model - obs).astype(jnp.bfloat16).astype(jnp.float32)
        residual = jnp.where(low, residual, 0.0)
        rows_r[u, EDGE : EDGE + STAMP, :] = residual
        rows_r[u, EDGE + STAMP : EDGE + 72, :] = jnp.zeros((8, LANES), jnp.float32)
        upper = pltpu.roll(rows_r[u, EDGE - 1 : EDGE + 71, :], STAMP, 1)
        rows_r[u, EDGE : EDGE + 72, :] = rows_r[u, EDGE : EDGE + 72, :] + upper
        stack = [
            rows_r[u, EDGE - 2 * m : EDGE - 2 * m + WIN, :].astype(jnp.bfloat16) for m in range(PAIRS)
        ]
        back = lax.dot_general(
            jnp.concatenate(stack, axis=1),
            banded[u],
            (((1,), (1,)), ((), ())),
            preferred_element_type=jnp.float32,
        )
        back = back.astype(jnp.bfloat16).astype(jnp.float32)
        back = jnp.concatenate([back, jnp.zeros((WIN, LANES - WPAD), jnp.float32)], axis=1)
        back = pltpu.roll(back, shift, 1)
        live = job < count
        begin = jnp.where(live, shift, LANES)
        end = jnp.where(live, shift, 0)
        total[b, tile, pl.ds(top, WIN), :] += jnp.where(lane_b >= begin, back, 0.0)
        total[b, after, pl.ds(top, WIN), :] += jnp.where(lane_b < end, back, 0.0)

    def step(index, carry):
        for u in range(TOGETHER):
            one(index * TOGETHER + u, u)
        return carry

    lax.fori_loop(0, lax.div(count + TOGETHER - 1, TOGETHER), step, 0)
    outs = [
        pltpu.make_async_copy(
            total.at[b, parity + t], out_hbm.at[b, :, pl.ds(t * LANES, LANES)], out_sems.at[b, t]
        )
        for b in range(bands)
        for t in range(OWN)
    ]
    for copy in outs:
        copy.start()
    for copy in outs:
        copy.wait()


def work(anchor, offsets, sky, halo, pieces, layout, slots, per_device):
    bands, rows_total = sky.shape[:2]
    smem = pl.BlockSpec(memory_space=pltpu.SMEM)
    anywhere = pl.BlockSpec(memory_space=pl.ANY)
    copies = 1 + OWN + sum(1 if masks is None else len(masks) for masks in layout)
    return pl.pallas_call(
        functools.partial(work_kernel, layout, slots, per_device),
        out_shape=jax.ShapeDtypeStruct((bands, rows_total, TILE), jnp.float32),
        in_specs=[smem, smem] + [anywhere] * (2 + len(pieces)),
        out_specs=anywhere,
        scratch_shapes=[
            pltpu.SMEM((4, bands * slots + TOGETHER), jnp.int32),
            pltpu.VMEM((bands, STRIP, rows_total + 16, LANES), jnp.bfloat16),
            pltpu.VMEM((bands, STRIP, rows_total, LANES), jnp.float32),
            pltpu.VMEM(halo.shape, jnp.bfloat16),
            pltpu.VMEM((slots, bands, ROWS, LANES), jnp.bfloat16),
            pltpu.VMEM((TOGETHER, WPAD + 16, LANES), jnp.float32),
            pltpu.VMEM((TOGETHER, WPAD, PAIRS * LANES), jnp.bfloat16),
            pltpu.VMEM((TOGETHER, PAIRS, WPAD, LANES), jnp.float32),
            pltpu.VMEM((TOGETHER, 72, LANES), jnp.float32),
            pltpu.VMEM((TOGETHER, 112, LANES), jnp.float32),
            pltpu.SemaphoreType.DMA((copies,)),
            pltpu.SemaphoreType.DMA((bands, OWN)),
        ],
        name="work",
    )(anchor, offsets, sky, halo, *pieces)


def on_device(sky, observed, psf, anchor, offsets):
    bands = sky.shape[0]
    per_device = observed.shape[1]
    n_sky = lax.axis_size("sky")
    n_exp = lax.axis_size("exp")
    slots = n_sky * n_exp
    both = ("sky", "exp")

    blocks, border = prep(sky, observed, psf)

    def across(x, mask):
        return lax.ppermute(x, both, [(i, i ^ mask) for i in range(slots)])

    if per_device == 1 and n_sky == 4 and n_exp == 2:
        far = across(blocks, 4)
        halo = lax.ppermute(border, "sky", [(s, s ^ 1) for s in range(n_sky)])
        own = jnp.concatenate([blocks, far], axis=0)
        pieces = [own]
        layout = [(0, 4)]
        for mask in (1, 2, 3):
            pieces.append(across(own, mask))
            layout.append((mask, mask ^ 4))
    else:
        halo = lax.ppermute(border, "sky", [(s, s ^ 1) for s in range(n_sky)])
        position = lax.axis_index("sky") * n_exp + lax.axis_index("exp")
        anchors = anchor.reshape(bands, slots, per_device)
        mine = lax.dynamic_index_in_dim(anchors, position, 1, keepdims=False)
        pair = 2 * jnp.arange(n_sky // 2, dtype=jnp.int32)[:, None, None]
        chosen = jnp.argmax(mine[None] == pair, axis=-1)
        picked = jnp.take_along_axis(blocks[None], chosen[:, None, :, None, None], axis=1)
        send = jnp.broadcast_to(picked, (n_sky // 2, 2 * n_exp, bands, ROWS, LANES))
        send = send.reshape(slots, bands, ROWS, LANES)
        pieces = [lax.all_to_all(send, both, 0, 0, tiled=True)]
        layout = [None]
    return work(anchor, offsets, sky, halo, pieces, layout, slots, per_device)


def solution(mesh):
    return jax.shard_map(
        on_device,
        mesh=mesh,
        in_specs=(
            P("band", None, ("group", "sky")),
            P("band", ("group", "sky", "exp"), None, None),
            P("band", ("group", "sky", "exp"), None),
            P("band", "group"),
            P("band", None, "group"),
        ),
        out_specs=P("band", None, ("group", "sky")),
        check_vma=False,
    )
```

time: 374 us -> 31 us (0.08); the launches traced: 369 us -> 31.4 us
  local copies, waits for them, and re-layouts: 201 us -> 3.43 us
  other arithmetic: 75 us -> 0 us
  waiting for transfers between devices: 67.2 us -> 6.44 us
  between operations: 13.5 us -> 0.05 us
  Pallas kernels: 0 us -> 12.2 us
    gather x81 -> x0, local copies, waits for them, and re-layouts: 114 us -> none
    scatter x24 -> x0, other arithmetic: 71.9 us -> none
    scatter x36 -> x0, local copies, waits for them, and re-layouts: 65.4 us -> none
    psum x1 -> x0, waiting for transfers between devices: 51.4 us -> none  [on_device(): return lax.psum(gradient, 'exp')]
    all_to_all x2 -> x0, waiting for transfers between devices: 15.8 us -> none  [the longest x1 8.8 us: on_device(): lax.all_to_all(pieces, 'sky', split_axis=0, concat_axis=0, tiled=True)]
    pallas_call x0 -> x2, Pallas kernels: none -> 12.2 us  [the longest x1 10.2 us: work(): pl.pallas_call(functools.partial(work_kernel, layout, slots, per_device),...]
    all_to_all x2 -> x0, starting transfers between devices: 9.8 us -> none  [the longest x1 6.35 us: on_device(): lax.all_to_all(pieces, 'sky', split_axis=0, concat_axis=0, tiled=True)]
    ppermute x0 -> x5, starting transfers between devices: none -> 9.26 us  [the longest x4 7.68 us: across(): return lax.ppermute(x, both, [(i, i ^ mask) for i in range(slots)])]
  transfers between devices with their start and end apart: 3 -> 5, of which waited for: 3 -> 2; matrix products, arithmetic and copies ran while one was open for 0% -> 2% of each run, Pallas kernels for 0% -> 0%
where the time goes in v1:
time: 31 us; the launch traced here: 31.4 us
  Pallas kernels  12.2 us (39%)
  starting transfers between devices  9.26 us (30%)
  waiting for transfers between devices  6.44 us (21%)
  local copies, waits for them, and re-layouts  3.43 us (11%)
    pallas_call x1, Pallas kernels, work(): pl.pallas_call(functools.partial(work_kernel, layout, slots, per_device),...  10.2 us
    ppermute x4, starting transfers between devices, across(): return lax.ppermute(x, both, [(i, i ^ mask) for i in range(slots)])  7.68 us
    ppermute x4, waiting for transfers between devices, across(): return lax.ppermute(x, both, [(i, i ^ mask) for i in range(slots)])  6.44 us
    unnamed x12, local copies, waits for them, and re-layouts  3.42 us
    pallas_call x1, Pallas kernels, prep(): pl.pallas_call(prep_kernel, out_shape=(jax.ShapeDtypeStruct((per_device,...  2.06 us
    ppermute x1, starting transfers between devices, on_device(): halo = lax.ppermute(border, 'sky', [(s, s ^ 1) for s in range(n_sky)])  1.58 us
  transfers between devices with their start and end apart: 5, of which 2 were waited for; matrix products, arithmetic and copies ran while one was open for 2% of the time, Pallas kernels for 0%

profile of v1, /device:TPU:0, one launch (start us, length us, event | category | flops | bytes accessed | tf_op | source)
XLA Modules:
  0.0 31.4 jit_solution(18208600600293704884)
XLA Ops:
  0.0 1.3 %copy.7.psf_hbm = bf16[3,1,625]{2,1,0:T(2,128)(2,1)} copy(bf16[3,1,625]{2,0,1:T(4,128)(2,1)} %param.8) | data formatting | bytes 7500 | tf_op args[2]
  1.3 2.1 %prep.1 = (bf16[1,3,48,128]{3,2,1,0:T(8,128)(2,1)}, bf16[3,128,384]{2,1,0:T(8,128)(2,1)}) custom-call(bf16[3,512,256]{2,1,0:T(8,128)(2,1)} %sky_hbm.3, bf16[625,128]{1,0:T(8,128)(2,1)} %constant.2.clone.table_hbm, bf16[3,1,64,64]{3,2,1,0:T(8,128)(2,1)} %obs_hbm.1, bf16[3,1,625]{2,1,0:T(2,128)(2,1)} %copy.7.psf_hbm), custom_call_target="tpu_custom_call" | custom-call | tf_op jit(solution)/shard_map/prep/pallas_call | solution.py:88
  3.4 4.1 %collective-permute-start.1 = (bf16[1,3,48,128]{3,2,1,0:T(8,128)(2,1)}, bf16[1,3,48,128]{3,2,1,0:T(8,128)(2,1)S(1)}, u32[]{:S(2)}, u32[]{:S(2)}) collective-permute-start(bf16[1,3,48,128]{3,2,1,0:T(8,128)(2,1)} %get-tuple-element.8), channel_id=1, source_target_pairs={{0,8},{2,10},{4,12},{6,14},{8,0},{10,2},{12,4},{14,6},{1,9},{3,11}... | collective-permute-start | bytes 110600 | tf_op jit(solution)/shard_map/ppermute | solution.py:308
  7.5 1.6 %collective-permute-start = (bf16[3,128,384]{2,1,0:T(8,128)(2,1)}, bf16[3,128,384]{2,1,0:T(8,128)(2,1)S(1)}, u32[]{:S(2)}, u32[]{:S(2)}) collective-permute-start(bf16[3,128,384]{2,1,0:T(8,128)(2,1)} %get-tuple-element.7), channel_id=1, source_target_pairs={{0,4},{4,0},{8,12},{12,8},{1,5},{5,1},{9,13},{13,9},{2,6},{6,2},{1... | collective-permute-start | bytes 884744 | tf_op jit(solution)/shard_map/ppermute | solution.py:312
  9.1 0.8 %constant_dynamic-update-slice_fusion.1 = bf16[2,3,48,128]{3,2,1,0:T(8,128)(2,1)S(1)} fusion(bf16[1,3,48,128]{3,2,1,0:T(8,128)(2,1)} %get-tuple-element.8), kind=kLoop, calls=%fused_computation.1 | loop fusion | bytes 73728
  9.8 0.3 collective-permute-done.1
  10.1 0.0 copy-start.1
  10.2 2.8 %collective-permute-start.4 = (bf16[2,3,48,128]{3,2,1,0:T(8,128)(2,1)S(1)}, bf16[2,3,48,128]{3,2,1,0:T(8,128)(2,1)S(1)}, u32[]{:S(2)}, u32[]{:S(2)}) collective-permute-start(bf16[2,3,48,128]{3,2,1,0:T(8,128)(2,1)S(1)} %constant_dynamic-update-slice_fusion.rest_0_), channel_id=1, source_target_pairs={{0,6},{2,4},{4,2},{6,0},{8,14},{10,12},{12,10},{14,8},{1,7},{3,5},... | collective-permute-start | bytes 221192 | tf_op jit(solution)/shard_map/ppermute | solution.py:308
  12.9 0.4 %collective-permute-start.3 = (bf16[2,3,48,128]{3,2,1,0:T(8,128)(2,1)S(1)}, bf16[2,3,48,128]{3,2,1,0:T(8,128)(2,1)S(1)}, u32[]{:S(2)}, u32[]{:S(2)}) collective-permute-start(bf16[2,3,48,128]{3,2,1,0:T(8,128)(2,1)S(1)} %constant_dynamic-update-slice_fusion.rest_0_), channel_id=1, source_target_pairs={{0,4},{2,6},{4,0},{6,2},{8,12},{10,14},{12,8},{14,10},{1,5},{3,7},... | collective-permute-start | bytes 221192 | tf_op jit(solution)/shard_map/ppermute | solution.py:308
  13.4 0.3 %collective-permute-start.2 = (bf16[2,3,48,128]{3,2,1,0:T(8,128)(2,1)S(1)}, bf16[2,3,48,128]{3,2,1,0:T(8,128)(2,1)S(1)}, u32[]{:S(2)}, u32[]{:S(2)}) collective-permute-start(bf16[2,3,48,128]{3,2,1,0:T(8,128)(2,1)S(1)} %constant_dynamic-update-slice_fusion.rest_0_), channel_id=1, source_target_pairs={{0,2},{2,0},{4,6},{6,4},{8,10},{10,8},{12,14},{14,12},{1,3},{3,1},... | collective-permute-start | bytes 221192 | tf_op jit(solution)/shard_map/ppermute | solution.py:308
  13.7 6.1 %collective-permute-done.4.rest_3_ = bf16[2,3,48,128]{3,2,1,0:T(8,128)(2,1)S(1)} collective-permute-done((bf16[2,3,48,128]{3,2,1,0:T(8,128)(2,1)S(1)}, bf16[2,3,48,128]{3,2,1,0:T(8,128)(2,1)S(1)}, u32[]{:S(2)}, u32[]{:S(2)}) %collective-permute-start.4) | collective-permute-done | bytes 73760 | tf_op jit(solution)/shard_map/ppermute | solution.py:308
  19.8 0.0 copy-start.2
  19.8 0.0 collective-permute-done.3.rest_2_
  19.8 0.0 copy-start.3
  19.8 0.0 collective-permute-done.2.rest_1_
  19.9 0.0 copy-start.4
  19.9 0.0 collective-permute-done.halo_hbm
  19.9 0.0 copy-done.1
  19.9 0.6 %copy-done.2 = bf16[2,3,48,128]{3,2,1,0:T(8,128)(2,1)} copy-done((bf16[2,3,48,128]{3,2,1,0:T(8,128)(2,1)}, bf16[2,3,48,128]{3,2,1,0:T(8,128)(2,1)S(1)}, u32[]{:S(2)}) %copy-start.2) | copy-done | bytes 73752
  20.5 0.0 copy-done.3
  20.5 0.0 copy-done.4
  20.5 0.0 copy-start
  20.5 0.7 %copy-done = bf16[3,128,384]{2,1,0:T(8,128)(2,1)} copy-done((bf16[3,128,384]{2,1,0:T(8,128)(2,1)}, bf16[3,128,384]{2,1,0:T(8,128)(2,1)S(1)}, u32[]{:S(2)}) %copy-start) | copy-done | bytes 294936
  21.2 10.2 %work.1 = f32[3,512,256]{2,1,0:T(8,128)} custom-call(s32[3,8]{1,0:T(4,128)} %anchor_ref.1, s32[3,2,8]{2,1,0:T(2,128)} %offset_ref.1, bf16[3,512,256]{2,1,0:T(8,128)(2,1)} %sky_hbm.3, bf16[3,128,384]{2,1,0:T(8,128)(2,1)} %copy-done, bf16[2,3,48,128]{3,2,1,0:T(8,128)(2,1)} %copy-done.1, bf16[2,3,48,128]{3,2,1,0:T(8,128)(2,1)} %copy-done.4, ...), custom_call_target="tpu_custom_call" | custom-call | tf_op jit(solution)/shard_map/work/pallas_call | solution.py:274
  (1 shorter events, 0.0 us)
Async XLA Ops:
  3.4 6.8 %collective-permute-start.1 = (bf16[1,3,48,128]{3,2,1,0:T(8,128)(2,1)}, bf16[1,3,48,128]{3,2,1,0:T(8,128)(2,1)S(1)}, u32[]{:S(2)}, u32[]{:S(2)}) collective-permute-start(bf16[1,3,48,128]{3,2,1,0:T(8,128)(2,1)} %get-tuple-element.8), channel_id=1, source_target_pairs={{0,8},{2,10},{4,12},{6,14},{8,0},{10,2},{12,4},{14,6},{1,9},{3,11}... | collective-permute-start | bytes 110600 | tf_op jit(solution)/shard_map/ppermute | solution.py:308
  7.5 12.4 %collective-permute-start = (bf16[3,128,384]{2,1,0:T(8,128)(2,1)}, bf16[3,128,384]{2,1,0:T(8,128)(2,1)S(1)}, u32[]{:S(2)}, u32[]{:S(2)}) collective-permute-start(bf16[3,128,384]{2,1,0:T(8,128)(2,1)} %get-tuple-element.7), channel_id=1, source_target_pairs={{0,4},{4,0},{8,12},{12,8},{1,5},{5,1},{9,13},{13,9},{2,6},{6,2},{1... | collective-permute-start | bytes 884744 | tf_op jit(solution)/shard_map/ppermute | solution.py:312
  10.1 9.7 %copy-start.1 = (bf16[2,3,48,128]{3,2,1,0:T(8,128)(2,1)}, bf16[2,3,48,128]{3,2,1,0:T(8,128)(2,1)S(1)}, u32[]{:S(2)}) copy-start(bf16[2,3,48,128]{3,2,1,0:T(8,128)(2,1)S(1)} %constant_dynamic-update-slice_fusion.rest_0_) | copy-start | bytes 221188
  10.2 9.7 %collective-permute-start.4 = (bf16[2,3,48,128]{3,2,1,0:T(8,128)(2,1)S(1)}, bf16[2,3,48,128]{3,2,1,0:T(8,128)(2,1)S(1)}, u32[]{:S(2)}, u32[]{:S(2)}) collective-permute-start(bf16[2,3,48,128]{3,2,1,0:T(8,128)(2,1)S(1)} %constant_dynamic-update-slice_fusion.rest_0_), channel_id=1, source_target_pairs={{0,6},{2,4},{4,2},{6,0},{8,14},{10,12},{12,10},{14,8},{1,7},{3,5},... | collective-permute-start | bytes 221192 | tf_op jit(solution)/shard_map/ppermute | solution.py:308
  12.9 6.9 %collective-permute-start.3 = (bf16[2,3,48,128]{3,2,1,0:T(8,128)(2,1)S(1)}, bf16[2,3,48,128]{3,2,1,0:T(8,128)(2,1)S(1)}, u32[]{:S(2)}, u32[]{:S(2)}) collective-permute-start(bf16[2,3,48,128]{3,2,1,0:T(8,128)(2,1)S(1)} %constant_dynamic-update-slice_fusion.rest_0_), channel_id=1, source_target_pairs={{0,4},{2,6},{4,0},{6,2},{8,12},{10,14},{12,8},{14,10},{1,5},{3,7},... | collective-permute-start | bytes 221192 | tf_op jit(solution)/shard_map/ppermute | solution.py:308
  13.4 6.5 %collective-permute-start.2 = (bf16[2,3,48,128]{3,2,1,0:T(8,128)(2,1)S(1)}, bf16[2,3,48,128]{3,2,1,0:T(8,128)(2,1)S(1)}, u32[]{:S(2)}, u32[]{:S(2)}) collective-permute-start(bf16[2,3,48,128]{3,2,1,0:T(8,128)(2,1)S(1)} %constant_dynamic-update-slice_fusion.rest_0_), channel_id=1, source_target_pairs={{0,2},{2,0},{4,6},{6,4},{8,10},{10,8},{12,14},{14,12},{1,3},{3,1},... | collective-permute-start | bytes 221192 | tf_op jit(solution)/shard_map/ppermute | solution.py:308
  19.8 0.6 %copy-start.2 = (bf16[2,3,48,128]{3,2,1,0:T(8,128)(2,1)}, bf16[2,3,48,128]{3,2,1,0:T(8,128)(2,1)S(1)}, u32[]{:S(2)}) copy-start(bf16[2,3,48,128]{3,2,1,0:T(8,128)(2,1)S(1)} %collective-permute-done.4.rest_3_) | copy-start | bytes 221188
  19.8 0.7 %copy-start.3 = (bf16[2,3,48,128]{3,2,1,0:T(8,128)(2,1)}, bf16[2,3,48,128]{3,2,1,0:T(8,128)(2,1)S(1)}, u32[]{:S(2)}) copy-start(bf16[2,3,48,128]{3,2,1,0:T(8,128)(2,1)S(1)} %collective-permute-done.3.rest_2_) | copy-start | bytes 221188
  19.9 0.7 %copy-start.4 = (bf16[2,3,48,128]{3,2,1,0:T(8,128)(2,1)}, bf16[2,3,48,128]{3,2,1,0:T(8,128)(2,1)S(1)}, u32[]{:S(2)}) copy-start(bf16[2,3,48,128]{3,2,1,0:T(8,128)(2,1)S(1)} %collective-permute-done.2.rest_1_) | copy-start | bytes 221188
  20.5 0.7 %copy-start = (bf16[3,128,384]{2,1,0:T(8,128)(2,1)}, bf16[3,128,384]{2,1,0:T(8,128)(2,1)S(1)}, u32[]{:S(2)}) copy-start(bf16[3,128,384]{2,1,0:T(8,128)(2,1)S(1)} %collective-permute-done.halo_hbm) | copy-start | bytes 884740

commit v2 on v1

v2 whole, which is shorter than its diff:
```python
import functools

import jax
import jax.numpy as jnp
from jax import lax
from jax.experimental import pallas as pl
from jax.experimental.pallas import tpu as pltpu
from jax.sharding import PartitionSpec as P

TILE = 256
PSF = 25
STAMP = 64
HALF = STAMP // 2
WIN = 88
LANES = 128
PAIRS = (PSF + 1) // 2
ROWS = 40
SHARED = 7
ASIDE = 32
WPAD = 96
OWN = TILE // LANES
STRIP = OWN + 1
EDGE = PSF - 1
FOLD = 4
TOGETHER = 2
FIELD = (9, 9, 7)
AHEAD = 1
PREP_VMEM = 40000 << 10


def lane_of(shape):
    return lax.broadcasted_iota(jnp.int32, shape, 1)


def row_of(shape):
    return lax.broadcasted_iota(jnp.int32, shape, 0)


def pack_into(blocks_ref, at, obs_ref, psf_ref, rows):
    bands, per_device = obs_ref.shape[:2]
    lines = bands * per_device
    taps = PSF * PSF
    lane = lane_of((lines, LANES))
    turn = (lane_of((LANES, LANES)) + row_of((LANES, LANES))) == LANES - 1
    turn = jnp.where(turn, 1.0, 0.0).astype(jnp.bfloat16)
    tiles = []
    for t in range(pl.cdiv(taps, LANES)):
        tile = psf_ref[:, t * LANES : min((t + 1) * LANES, taps)]
        if tile.shape[1] < LANES:
            tile = jnp.concatenate([tile, jnp.zeros((lines, LANES - tile.shape[1]), tile.dtype)], axis=1)
        tiles.append(jnp.dot(tile, turn, preferred_element_type=jnp.float32))

    def run(first, target, count=PSF):
        t, end = first // LANES, (first + count - 1) // LANES
        value = tiles[t] if end == t else jnp.where(lane < LANES // 2, tiles[t], tiles[end])
        value = pltpu.roll(value, (target + first + 1) % LANES, 1)
        return jnp.where(jnp.bitwise_and(target - lane, LANES - 1) < count, value, 0.0)

    for r in range(8):
        row = jnp.zeros((lines, LANES), jnp.float32)
        for m, aside in ((r, 0), (r + SHARED, ASIDE)):
            if r < SHARED and m < PAIRS:
                row = row + run(2 * PSF * m, aside)
                if 2 * m + 1 < PSF:
                    row = row + run(2 * PSF * m + PSF, aside + STAMP)
        rows[r] = row
    for x in range(per_device):
        for b in range(bands):
            stamp = obs_ref[b, x].astype(jnp.float32)
            both = jnp.concatenate([stamp[:HALF], stamp[HALF:]], axis=1)
            blocks_ref[at + x, b, 0:HALF, :] = both.astype(jnp.bfloat16)
            blocks_ref[at + x, b, HALF:ROWS, :] = rows[:, b * per_device + x, :].astype(jnp.bfloat16)


def prep_kernel(sky_hbm, obs_hbm, psf_hbm, first_ref, second_ref, blocks_ref, edge, obs, psf, rows, sems):
    bands, rows_total = sky_hbm.shape[:2]
    parity = lax.axis_index("sky") % 2
    side = pl.multiple_of((1 - parity) * (TILE - LANES), LANES)
    copies = [
        pltpu.make_async_copy(sky_hbm.at[b, :, pl.ds(side, LANES)], edge.at[b], sems.at[b]) for b in range(bands)
    ]
    copies.append(pltpu.make_async_copy(psf_hbm, psf, sems.at[bands]))
    copies.append(pltpu.make_async_copy(obs_hbm, obs, sems.at[bands + 1]))
    for copy in copies:
        copy.start()
    fold = rows_total // FOLD
    lane = lane_of((fold, LANES))
    base = (1 - parity) * WIN
    for b in range(bands):
        copies[b].wait()
        turned = []
        for g in range(FOLD):
            part = edge[b, g * fold : (g + 1) * fold, :].astype(jnp.float32)
            turned.append(pltpu.roll(part, (base + WIN * g) % LANES, 1))
        dst = first_ref.at[b] if b < AHEAD else second_ref.at[b - AHEAD]
        for t in range(STRIP):
            limit = WIN * (t + 1) - LANES * t
            tile = jnp.where(lane < limit, turned[t], turned[t + 1])
            dst[:, t * LANES : (t + 1) * LANES] = tile.astype(jnp.bfloat16)
    for copy in copies[bands:]:
        copy.wait()
    pack_into(blocks_ref, 0, obs, psf, rows)


def prep(sky, observed, psf):
    bands, rows_total = sky.shape[:2]
    per_device = observed.shape[1]
    shape = (rows_total // FOLD, STRIP * LANES)
    hbm = pl.BlockSpec(memory_space=pltpu.HBM)
    vmem = pl.BlockSpec(memory_space=pltpu.VMEM)
    return pl.pallas_call(
        prep_kernel,
        out_shape=(
            jax.ShapeDtypeStruct((AHEAD,) + shape, jnp.bfloat16),
            jax.ShapeDtypeStruct((bands - AHEAD,) + shape, jnp.bfloat16),
            jax.ShapeDtypeStruct((per_device, bands, ROWS, LANES), jnp.bfloat16),
        ),
        in_specs=[hbm] * 3,
        out_specs=(vmem,) * 3,
        scratch_shapes=[
            pltpu.VMEM((bands, rows_total, LANES), jnp.bfloat16),
            pltpu.VMEM(observed.shape, jnp.bfloat16),
            pltpu.VMEM(psf.shape, jnp.bfloat16),
            pltpu.VMEM((8, bands * per_device, LANES), jnp.float32),
            pltpu.SemaphoreType.DMA((bands + 2,)),
        ],
        compiler_params=pltpu.CompilerParams(vmem_limit_bytes=PREP_VMEM),
        cost_estimate=pl.CostEstimate(flops=0, bytes_accessed=1 << 20, transcendentals=0),
        name="prep",
    )(sky, observed, psf)


def merge_kernel(own_ref, obs_ref, psf_ref, both_ref, rows):
    both_ref[0:1] = own_ref[...]
    pack_into(both_ref, 1, obs_ref, psf_ref, rows)


def merge(own, observed, psf):
    vmem = pl.BlockSpec(memory_space=pltpu.VMEM)
    return pl.pallas_call(
        merge_kernel,
        out_shape=jax.ShapeDtypeStruct((2 * own.shape[0],) + own.shape[1:], jnp.bfloat16),
        in_specs=[vmem] * 3,
        out_specs=vmem,
        scratch_shapes=[pltpu.VMEM((8, psf.shape[0], LANES), jnp.float32)],
        compiler_params=pltpu.CompilerParams(vmem_limit_bytes=8 << 20),
        cost_estimate=pl.CostEstimate(flops=0, bytes_accessed=1 << 20, transcendentals=0),
        name="merge",
    )(own, observed, psf)


def plan_kernel(bands, anchor_ref, offset_ref, plan_ref):
    column = lax.axis_index("sky")
    parity = column % 2
    first = column - parity
    crossing = TILE - WIN
    slots = lax.axis_size("sky") * lax.axis_size("exp")
    per_device = anchor_ref.shape[1] // slots
    cap = plan_ref.shape[1]
    low = jnp.where(parity == 0, -1, crossing)
    high = jnp.where(parity == 0, TILE, 2 * TILE)
    aside = parity * (TILE - LANES)

    def code_of(b, n, top, start):
        code = jnp.int32(b << (FIELD[0] + FIELD[1] + FIELD[2]))
        return code + (n << (FIELD[0] + FIELD[1])) + (top << FIELD[1]) + start

    def visit(b, n, counts):
        early, late = counts
        for x in range(per_device):
            i = n * per_device + x
            left = offset_ref[b, 1, i]
            meets = (anchor_ref[b, i] == first) & (left > low) & (left < high)
            code = code_of(b, n, offset_ref[b, 0, i], left - aside)
            if b < AHEAD:
                plan_ref[0, early] = code
                early = early + meets.astype(jnp.int32)
            else:
                later = meets & (left > crossing) & (left < TILE)
                plan_ref[0, early] = code
                plan_ref[1, late] = code
                late = late + later.astype(jnp.int32)
                early = early + (meets.astype(jnp.int32) - later.astype(jnp.int32))
        return early, late

    counts = (jnp.int32(0), jnp.int32(0))
    for b in range(bands):
        if slots <= 8:
            for n in range(slots):
                counts = visit(b, jnp.int32(n), counts)
        else:
            counts = lax.fori_loop(0, slots, functools.partial(visit, b), counts)
    for k in range(2):
        for extra in range(TOGETHER):
            plan_ref[k, counts[k] + extra] = code_of(bands - 1, jnp.int32(0), jnp.int32(0), jnp.int32(LANES))
        plan_ref[k, cap - 1] = counts[k]


def make_plan(anchor, offsets, slots):
    bands = anchor.shape[0]
    smem = pl.BlockSpec(memory_space=pltpu.SMEM)
    return pl.pallas_call(
        functools.partial(plan_kernel, bands),
        out_shape=jax.ShapeDtypeStruct((2, bands * slots + TOGETHER + 2), jnp.int32),
        in_specs=[smem] * 2,
        out_specs=smem,
        compiler_params=pltpu.CompilerParams(vmem_limit_bytes=8 << 20),
        cost_estimate=pl.CostEstimate(flops=0, bytes_accessed=1 << 20, transcendentals=0),
        name="plan",
    )(anchor, offsets)


def unfold(strip, b, tile, halo, place, rows_total):
    fold = rows_total // FOLD
    lane = jnp.bitwise_and(lane_of((fold, LANES)) - place, LANES - 1)
    tiles = [halo[:, t * LANES : (t + 1) * LANES].astype(jnp.float32) for t in range(STRIP)]
    for g in range(FOLD):
        shift = (place + LANES - WIN * g % LANES) % LANES
        first = WIN * g // LANES
        limit = LANES * (first + 1) - WIN * g
        value = pltpu.roll(tiles[first], shift, 1)
        if limit < WIN:
            value = jnp.where(lane < limit, value, pltpu.roll(tiles[first + 1], shift, 1))
        strip[b, tile, g * fold : (g + 1) * fold, :] = value.astype(jnp.bfloat16)


def work_kernel(late, layout, plan_ref, sky_hbm, halo, *rest):
    pieces = rest[: len(layout)]
    rest = rest[len(layout) + late :]
    out_hbm, strip, total, blocks, cut, view, banded, wide, rows_a, rows_r, sems, out_sems = rest
    bands, rows_total = sky_hbm.shape[:2]
    column = lax.axis_index("sky")
    parity = column % 2
    position = column * lax.axis_size("exp") + lax.axis_index("exp")
    border_tile = OWN * (1 - parity)
    mine = list(range(AHEAD if late else 0, bands))
    own = [1 - parity] if late else list(range(OWN))

    def tile_copy(b, t, k):
        side = pl.multiple_of(t * LANES, LANES)
        return pltpu.make_async_copy(
            sky_hbm.at[b, :, pl.ds(side, LANES)], strip.at[b, parity + t, pl.ds(0, rows_total), :], sems.at[b, k]
        )

    def total_copy(b, t, k, inward):
        side = pl.multiple_of(t * LANES, LANES)
        here, there = total.at[b, parity + t], out_hbm.at[b, :, pl.ds(side, LANES)]
        if inward:
            return pltpu.make_async_copy(there, here, out_sems.at[b, k])
        return pltpu.make_async_copy(here, there, out_sems.at[b, k])

    copies = [tile_copy(b, t, k) for b in mine for k, t in enumerate(own)]
    if late:
        copies += [total_copy(b, t, k, True) for b in mine for k, t in enumerate(own)]
    for copy in copies:
        copy.start()
    for masks, piece in zip(layout, pieces):
        if masks is not None:
            for j, mask in enumerate(masks):
                blocks[jnp.bitwise_xor(position, mask)] = piece[j]
        else:
            blocks = piece

    mode = int(late)
    count = plan_ref[mode, plan_ref.shape[1] - 1]
    rows_r[...] = jnp.zeros(rows_r.shape, jnp.float32)
    for b in mine:
        if not late:
            for t in range(OWN):
                total[b, parity + t] = jnp.zeros((rows_total, LANES), jnp.float32)
            if b >= AHEAD:
                strip[b, border_tile, 0:rows_total, :] = jnp.zeros((rows_total, LANES), jnp.bfloat16)
        for t in range(STRIP):
            strip[b, t, rows_total : rows_total + 16, :] = jnp.zeros((16, LANES), jnp.bfloat16)
    for k, b in enumerate(mine if late else range(AHEAD)):
        unfold(strip, b, border_tile, halo[k], parity * (LANES - WIN), rows_total)
    for copy in copies:
        copy.wait()

    lane_w = lane_of((WPAD, LANES))
    gap = row_of((WPAD, LANES)) - lane_w % STAMP
    inside = (gap >= 0) & (gap < PSF) & (row_of((WPAD, LANES)) < WIN)
    lane_c = lane_of((WPAD + 16, LANES))
    lane_b = lane_of((WIN, LANES))
    low = lane_of((STAMP, LANES)) < STAMP

    def where_is(job):
        code = plan_ref[mode, job]
        n = jnp.bitwise_and(lax.shift_right_logical(code, FIELD[0] + FIELD[1]), (1 << FIELD[2]) - 1)
        return lax.shift_right_logical(code, FIELD[0] + FIELD[1] + FIELD[2]), n, code

    def fields(job):
        b, n, code = where_is(job)
        top = jnp.bitwise_and(lax.shift_right_logical(code, FIELD[1]), (1 << FIELD[0]) - 1)
        start = jnp.bitwise_and(code, (1 << FIELD[1]) - 1)
        tile = lax.shift_right_logical(start, 7)
        shift = jnp.bitwise_and(start, LANES - 1)
        after = jnp.minimum(tile + 1, STRIP - 1)
        return b, n, top, tile, after, shift

    def load_window(job, u):
        b, _, top, tile, after, shift = fields(job)
        back_shift = jnp.bitwise_and(LANES - shift, LANES - 1)
        base = pl.multiple_of(jnp.bitwise_and(top, -16), 16)
        left = pltpu.roll(strip[b, tile, pl.ds(base, WPAD + 16), :].astype(jnp.float32), back_shift, 1)
        right = pltpu.roll(strip[b, after, pl.ds(base, WPAD + 16), :].astype(jnp.float32), back_shift, 1)
        cut[u] = jnp.where(lane_c < LANES - shift, left, right)
        view[u] = cut[u, pl.ds(top - base, WPAD), :].astype(jnp.bfloat16)

    def build(job, u, first, last):
        b, n, _ = where_is(job)
        taps = blocks[n, b, HALF:ROWS, :].astype(jnp.float32)
        for m in range(first, min(last, PAIRS)):
            row = m % SHARED
            spread = jnp.broadcast_to(taps[row : row + 1, :], (WPAD, LANES))
            offset = 0 if m < SHARED else LANES - ASIDE
            turned = pltpu.roll(spread, offset, 1, stride=1, stride_axis=0)
            banded[u, :, m * LANES : (m + 1) * LANES] = jnp.where(inside, turned, 0.0).astype(jnp.bfloat16)

    def forward(u, first, last):
        last = min(last, PAIRS)
        product = jnp.dot(
            view[u, :, :WPAD],
            banded[u, :, first * LANES : last * LANES],
            preferred_element_type=jnp.float32,
        )
        for m in range(first, last):
            wide[u, m] = product[:, (m - first) * LANES : (m - first + 1) * LANES]

    def residual(job, u):
        b, n, _ = where_is(job)
        acc = wide[u, 0, 0:72, :]
        for m in range(1, PAIRS):
            acc = acc + wide[u, m, 2 * m : 2 * m + 72, :]
        rows_a[u] = acc
        model = rows_a[u, 0:STAMP, :] + pltpu.roll(rows_a[u, 1 : STAMP + 1, :], STAMP, 1)
        obs = blocks[n, b, 0:HALF, :].astype(jnp.float32)
        obs = jnp.concatenate([obs, pltpu.roll(obs, STAMP, 1)], axis=0)
        rest = (model - obs).astype(jnp.bfloat16).astype(jnp.float32)
        rest = jnp.where(low, rest, 0.0)
        rows_r[u, EDGE : EDGE + STAMP, :] = rest
        rows_r[u, EDGE + STAMP : EDGE + 72, :] = jnp.zeros((8, LANES), jnp.float32)
        upper = pltpu.roll(rows_r[u, EDGE - 1 : EDGE + 71, :], STAMP, 1)
        rows_r[u, EDGE : EDGE + 72, :] = rows_r[u, EDGE : EDGE + 72, :] + upper

    def backward(u):
        stack = [
            rows_r[u, EDGE - 2 * m : EDGE - 2 * m + WIN, :].astype(jnp.bfloat16) for m in range(PAIRS)
        ]
        back = lax.dot_general(
            jnp.concatenate(stack, axis=1),
            banded[u],
            (((1,), (1,)), ((), ())),
            preferred_element_type=jnp.float32,
        )
        back = back.astype(jnp.bfloat16).astype(jnp.float32)
        return jnp.concatenate([back, jnp.zeros((WIN, LANES - WPAD), jnp.float32)], axis=1)

    def add(job, back):
        b, _, top, tile, after, shift = fields(job)
        back = pltpu.roll(back, shift, 1)
        live = job < count
        begin = jnp.where(live, shift, LANES)
        end = jnp.where(live, shift, 0)
        if late:
            from_left = jnp.where(parity == 0, begin, LANES)
            to_right = jnp.where(parity == 0, 0, end)
            part = jnp.where((lane_b >= from_left) | (lane_b < to_right), back, 0.0)
            total[b, 1, pl.ds(top, WIN), :] += part
        else:
            total[b, tile, pl.ds(top, WIN), :] += jnp.where(lane_b >= begin, back, 0.0)
            total[b, after, pl.ds(top, WIN), :] += jnp.where(lane_b < end, back, 0.0)

    outs = {b: [total_copy(b, t, k, False) for k, t in enumerate(own)] for b in mine}

    def flush(b, ready):
        @pl.when(ready)
        def _():
            for copy in outs[b]:
                copy.start()

    def step(index, before):
        one = index * 2
        two = one + 1
        now = where_is(one)[0]
        for b in mine[:-1]:
            flush(b, (before <= b) & (now > b))
        load_window(two, 1)
        for c in range(0, PAIRS, 2):
            forward(0, c, c + 2)
            build(two, 1, c, c + 2)
        residual(one, 0)
        for c in range(0, PAIRS, 2):
            forward(1, c, c + 2)
        back_one = backward(0)
        residual(two, 1)
        back_two = backward(1)
        add(one, back_one)
        load_window(one + 2, 0)
        build(one + 2, 0, 0, PAIRS)
        add(two, back_two)
        return now

    load_window(0, 0)
    build(0, 0, 0, PAIRS)
    before = lax.fori_loop(0, lax.div(count + 1, 2), step, jnp.int32(0))
    for b in mine:
        flush(b, before <= b)
    for b in mine:
        for copy in outs[b]:
            copy.wait()


def work(late, plan, sky, halo, pieces, layout, slots, so_far=None):
    bands, rows_total = sky.shape[:2]
    smem = pl.BlockSpec(memory_space=pltpu.SMEM)
    hbm = pl.BlockSpec(memory_space=pltpu.HBM)
    vmem = pl.BlockSpec(memory_space=pltpu.VMEM)
    gathered = (slots, bands, ROWS, LANES) if layout[0] is not None else (1, 1, 8, LANES)
    extra = [so_far] if late else []
    return pl.pallas_call(
        functools.partial(work_kernel, late, layout),
        out_shape=jax.ShapeDtypeStruct((bands, rows_total, TILE), jnp.float32),
        in_specs=[smem, hbm] + [vmem] * (1 + len(pieces)) + [hbm] * len(extra),
        out_specs=hbm,
        scratch_shapes=[
            pltpu.VMEM((bands, STRIP, rows_total + 16, LANES), jnp.bfloat16),
            pltpu.VMEM((bands, STRIP, rows_total, LANES), jnp.float32),
            pltpu.VMEM(gathered, jnp.bfloat16),
            pltpu.VMEM((TOGETHER, WPAD + 16, LANES), jnp.float32),
            pltpu.VMEM((TOGETHER, WPAD, LANES), jnp.bfloat16),
            pltpu.VMEM((TOGETHER, WPAD, PAIRS * LANES), jnp.bfloat16),
            pltpu.VMEM((TOGETHER, PAIRS, WPAD, LANES), jnp.float32),
            pltpu.VMEM((TOGETHER, 72, LANES), jnp.float32),
            pltpu.VMEM((TOGETHER, 112, LANES), jnp.float32),
            pltpu.SemaphoreType.DMA((bands, OWN)),
            pltpu.SemaphoreType.DMA((bands, OWN)),
        ],
        compiler_params=pltpu.CompilerParams(vmem_limit_bytes=24 << 20),
        cost_estimate=pl.CostEstimate(flops=0, bytes_accessed=8 << 20, transcendentals=0),
        input_output_aliases={3 + len(pieces): 0} if late else {},
        name="late" if late else "early",
    )(plan, sky, halo, *pieces, *extra)


def on_device(sky, observed, psf, anchor, offsets):
    bands = sky.shape[0]
    per_device = observed.shape[1]
    n_sky = lax.axis_size("sky")
    n_exp = lax.axis_size("exp")
    slots = n_sky * n_exp
    both = ("sky", "exp")
    taps = psf.reshape(bands * per_device, psf.shape[-1])
    direct = per_device == 1 and n_sky == 4 and n_exp == 2

    def across(x, mask):
        return lax.ppermute(x, both, [(i, i ^ mask) for i in range(slots)])

    def neighbour(x):
        return lax.ppermute(x, "sky", [(s, s ^ 1) for s in range(n_sky)])

    if direct:
        far_observed = across(observed, 4)
        far_taps = across(taps, 4)
    first, second, blocks = prep(sky, observed, taps)
    halo_first = neighbour(first)
    if direct:
        own = merge(blocks, far_observed, far_taps)
        pieces = [own]
        layout = [(0, 4)]
        for mask in (2, 3, 1):
            pieces.append(across(own, mask))
            layout.append((mask, mask ^ 4))
    else:
        position = lax.axis_index("sky") * n_exp + lax.axis_index("exp")
        anchors = anchor.reshape(bands, slots, per_device)
        mine = lax.dynamic_index_in_dim(anchors, position, 1, keepdims=False)
        pair = 2 * jnp.arange(n_sky // 2, dtype=jnp.int32)[:, None, None]
        chosen = jnp.argmax(mine[None] == pair, axis=-1)
        picked = jnp.take_along_axis(blocks[None], chosen[:, None, :, None, None], axis=1)
        send = jnp.broadcast_to(picked, (n_sky // 2, 2 * n_exp, bands, ROWS, LANES))
        send = send.reshape(slots, bands, ROWS, LANES)
        pieces = [lax.all_to_all(send, both, 0, 0, tiled=True)]
        layout = [None]
    halo_second = neighbour(second)
    plan = make_plan(anchor, offsets, slots)
    so_far = work(False, plan, sky, halo_first, pieces, layout, slots)
    return work(True, plan, sky, halo_second, pieces, layout, slots, so_far)


def solution(mesh):
    return jax.shard_map(
        on_device,
        mesh=mesh,
        in_specs=(
            P("band", None, ("group", "sky")),
            P("band", ("group", "sky", "exp"), None, None),
            P("band", ("group", "sky", "exp"), None),
            P("band", "group"),
            P("band", None, "group"),
        ),
        out_specs=P("band", None, ("group", "sky")),
        check_vma=False,
    )
```

time: 31 us -> 33.2 us (1.071); the launches traced: 31.4 us -> 32.9 us
  starting transfers between devices: 9.26 us -> 11 us
  local copies, waits for them, and re-layouts: 3.43 us -> 3.98 us
  waiting for transfers between devices: 6.44 us -> 5.99 us
  Pallas kernels: 12.2 us -> 11.8 us
    ppermute x1 -> x2, starting transfers between devices: 1.58 us -> 3.2 us  [neighbour(): return lax.ppermute(x, 'sky', [(s, s ^ 1) for s in range(n_sky)])]
    unnamed x12 -> x10, local copies, waits for them, and re-layouts: 3.42 us -> 3.98 us
    ppermute x4 -> x5, waiting for transfers between devices: 6.44 us -> 5.99 us  [across(): return lax.ppermute(x, both, [(i, i ^ mask) for i in range(slots)])]
    pallas_call x2 -> x5, Pallas kernels: 12.2 us -> 11.8 us  [the longest x2 9.39 us: work(): pl.pallas_call(functools.partial(work_kernel, late, layout), out_shape=ja...]
    ppermute x4 -> x5, starting transfers between devices: 7.68 us -> 7.81 us  [across(): return lax.ppermute(x, both, [(i, i ^ mask) for i in range(slots)])]
  transfers between devices with their start and end apart: 5 -> 7, of which waited for: 2 -> 2; matrix products, arithmetic and copies ran while one was open for 2% -> 0% of each run, Pallas kernels for 0% -> 22%
where the time goes in v2:
time: 33.2 us; the launch traced here: 32.9 us
  Pallas kernels  11.8 us (36%)
  starting transfers between devices  11 us (33%)
  waiting for transfers between devices  5.99 us (18%)
  local copies, waits for them, and re-layouts  3.98 us (12%)
    pallas_call x2, Pallas kernels, work(): pl.pallas_call(functools.partial(work_kernel, late, layout), out_shape=ja...  9.39 us
    ppermute x5, starting transfers between devices, across(): return lax.ppermute(x, both, [(i, i ^ mask) for i in range(slots)])  7.81 us
    ppermute x5, waiting for transfers between devices, across(): return lax.ppermute(x, both, [(i, i ^ mask) for i in range(slots)])  5.99 us
    unnamed x10, local copies, waits for them, and re-layouts  3.98 us
    ppermute x2, starting transfers between devices, neighbour(): return lax.ppermute(x, 'sky', [(s, s ^ 1) for s in range(n_sky)])  3.2 us
    pallas_call x1, Pallas kernels, make_plan(): pl.pallas_call(functools.partial(plan_kernel, bands), out_shape=jax.Shape...  1.41 us
    pallas_call x1, Pallas kernels, prep(): pl.pallas_call(prep_kernel, out_shape=(jax.ShapeDtypeStruct((AHEAD,) + sh...  0.76 us
  transfers between devices with their start and end apart: 7, of which 2 were waited for; matrix products, arithmetic and copies ran while one was open for 0% of the time, Pallas kernels for 22%

profile of v2, /device:TPU:0, one launch (start us, length us, event | category | flops | bytes accessed | tf_op | source)
XLA Modules:
  0.0 32.9 jit_solution(6095921730193745892)
XLA Ops:
  0.0 0.0 copy-start
  0.0 1.1 %copy-done = bf16[3,512,256]{2,1,0:T(8,128)(2,1)S(1)} copy-done((bf16[3,512,256]{2,1,0:T(8,128)(2,1)S(1)}, bf16[3,512,256]{2,1,0:T(8,128)(2,1)}, u32[]{:S(2)}) %copy-start) | copy-done | bytes 786456
  1.1 0.0 copy-start.1
  1.1 0.8 %copy-done.1 = bf16[3,1,64,64]{3,2,1,0:T(8,128)(2,1)S(1)} copy-done((bf16[3,1,64,64]{3,2,1,0:T(8,128)(2,1)S(1)}, bf16[3,1,64,64]{3,2,1,0:T(8,128)(2,1)}, u32[]{:S(2)}) %copy-start.1) | copy-done | bytes 24600
  1.9 0.0 copy-start.2
  1.9 0.7 %copy-done.2 = bf16[3,1,625]{2,0,1:T(4,128)(2,1)S(1)} copy-done((bf16[3,1,625]{2,0,1:T(4,128)(2,1)S(1)}, bf16[3,1,625]{2,0,1:T(4,128)(2,1)}, u32[]{:S(2)}) %copy-start.2) | copy-done | bytes 3774
  2.6 0.8 %prep.1 = (bf16[1,128,384]{2,1,0:T(8,128)(2,1)S(1)}, bf16[2,128,384]{2,1,0:T(8,128)(2,1)S(1)}, bf16[1,3,40,128]{3,2,1,0:T(8,128)(2,1)S(1)}) custom-call(bf16[3,512,256]{2,1,0:T(8,128)(2,1)S(1)} %copy-done, bf16[3,1,64,64]{3,2,1,0:T(8,128)(2,1)S(1)} %copy-done.1, bf16[3,625]{1,0:T(4,128)(2,1)S(1)} %bitcast.1), custom_call_target="tpu_custom_call" | custom-call | bytes 1048576 | tf_op jit(solution)/shard_map/prep/pallas_call | solution.py:111
  3.4 3.1 %collective-permute-start = (bf16[2,128,384]{2,1,0:T(8,128)(2,1)S(1)}, bf16[2,128,384]{2,1,0:T(8,128)(2,1)S(1)}, u32[]{:S(2)}, u32[]{:S(2)}) collective-permute-start(bf16[2,128,384]{2,1,0:T(8,128)(2,1)S(1)} %get-tuple-element.8), channel_id=1, source_target_pairs={{0,4},{4,0},{8,12},{12,8},{1,5},{5,1},{9,13},{13,9},{2,6},{6,2},{1... | collective-permute-start | bytes 589832 | tf_op jit(solution)/shard_map/ppermute | solution.py:460
  6.5 0.1 collective-permute-start.6
  6.6 3.0 %collective-permute-start.1 = (bf16[3,1,64,64]{3,2,1,0:T(8,128)(2,1)S(1)}, bf16[3,1,64,64]{3,2,1,0:T(8,128)(2,1)S(1)}, u32[]{:S(2)}, u32[]{:S(2)}) collective-permute-start(bf16[3,1,64,64]{3,2,1,0:T(8,128)(2,1)S(1)} %copy-done.1), channel_id=1, source_target_pairs={{0,8},{2,10},{4,12},{6,14},{8,0},{10,2},{12,4},{14,6},{1,9},{3,11}... | collective-permute-start | bytes 73736 | tf_op jit(solution)/shard_map/ppermute | solution.py:457
  9.5 0.0 collective-permute-start.2
  9.6 4.6 %collective-permute-done.2.psf_ref = bf16[3,625]{1,0:T(4,128)(2,1)S(1)} collective-permute-done((bf16[3,625]{1,0:T(4,128)(2,1)S(1)}, bf16[3,625]{1,0:T(4,128)(2,1)S(1)}, u32[]{:S(2)}, u32[]{:S(2)}) %collective-permute-start.2) | collective-permute-done | bytes 3782 | tf_op jit(solution)/shard_map/ppermute | solution.py:457
  14.2 0.0 collective-permute-done.1.obs_ref
  14.2 0.3 merge.1.rest_0_
  14.4 1.6 %collective-permute-start.5 = (bf16[2,3,40,128]{3,2,1,0:T(8,128)(2,1)S(1)}, bf16[2,3,40,128]{3,2,1,0:T(8,128)(2,1)S(1)}, u32[]{:S(2)}, u32[]{:S(2)}) collective-permute-start(bf16[2,3,40,128]{3,2,1,0:T(8,128)(2,1)S(1)} %merge.1.rest_0_), channel_id=1, source_target_pairs={{0,2},{2,0},{4,6},{6,4},{8,10},{10,8},{12,14},{14,12},{1,3},{3,1},... | collective-permute-start | bytes 184328 | tf_op jit(solution)/shard_map/ppermute | solution.py:457
  16.0 3.2 %collective-permute-start.4 = (bf16[2,3,40,128]{3,2,1,0:T(8,128)(2,1)S(1)}, bf16[2,3,40,128]{3,2,1,0:T(8,128)(2,1)S(1)}, u32[]{:S(2)}, u32[]{:S(2)}) collective-permute-start(bf16[2,3,40,128]{3,2,1,0:T(8,128)(2,1)S(1)} %merge.1.rest_0_), channel_id=1, source_target_pairs={{0,6},{2,4},{4,2},{6,0},{8,14},{10,12},{12,10},{14,8},{1,7},{3,5},... | collective-permute-start | bytes 184328 | tf_op jit(solution)/shard_map/ppermute | solution.py:457
  19.2 0.0 collective-permute-start.3
  19.3 0.0 copy-start.3
  19.3 0.7 %copy-done.3 = s32[3,2,8]{2,1,0:T(2,128)S(1)} copy-done((s32[3,2,8]{2,1,0:T(2,128)S(1)}, s32[3,2,8]{2,1,0:T(2,128)}, u32[]{:S(2)}) %copy-start.3) | copy-done | bytes 216
  19.9 0.0 copy-start.4
  19.9 0.7 %copy-done.4 = s32[3,8]{1,0:T(4,128)S(1)} copy-done((s32[3,8]{1,0:T(4,128)S(1)}, s32[3,8]{1,0:T(4,128)}, u32[]{:S(2)}) %copy-start.4) | copy-done | bytes 120
  20.6 1.4 %plan.1.plan_ref = s32[2,28]{1,0:T(2,128)S(1)} custom-call(s32[3,8]{1,0:T(4,128)S(1)} %copy-done.4, s32[3,2,8]{2,1,0:T(2,128)S(1)} %copy-done.3), custom_call_target="tpu_custom_call" | custom-call | bytes 1048576 | tf_op jit(solution)/shard_map/plan/pallas_call | solution.py:202
  22.0 0.0 collective-permute-done.5.rest_3_
  22.1 0.0 collective-permute-done.4.rest_2_
  22.1 1.4 %collective-permute-done.3.rest_1_ = bf16[2,3,40,128]{3,2,1,0:T(8,128)(2,1)S(1)} collective-permute-done((bf16[2,3,40,128]{3,2,1,0:T(8,128)(2,1)S(1)}, bf16[2,3,40,128]{3,2,1,0:T(8,128)(2,1)S(1)}, u32[]{:S(2)}, u32[]{:S(2)}) %collective-permute-start.3) | collective-permute-done | bytes 61472 | tf_op jit(solution)/shard_map/ppermute | solution.py:457
  23.5 0.0 collective-permute-done.6.halo
  23.5 5.7 %early.1.rest_4_ = f32[3,512,256]{2,1,0:T(8,128)} custom-call(s32[2,28]{1,0:T(2,128)S(1)} %plan.1.plan_ref, bf16[3,512,256]{2,1,0:T(8,128)(2,1)S(1)} %copy-done, bf16[1,128,384]{2,1,0:T(8,128)(2,1)S(1)} %collective-permute-done.6.halo, bf16[2,3,40,128]{3,2,1,0:T(8,128)(2,1)S(1)} %merge.1.rest_0_, bf16[2,3,40,128]{3,2,1,0:T(8,128)(2,1)S(1)} %collective-permute-done.3.rest_1_, ...), custom_call_target="tpu_custom_call" | custom-call | bytes 8388608 | tf_op jit(solution)/shard_map/early/pallas_call | solution.py:421
  29.1 0.0 collective-permute-done.halo
  29.1 3.7 %late.1 = f32[3,512,256]{2,1,0:T(8,128)} custom-call(s32[2,28]{1,0:T(2,128)S(1)} %plan.1.plan_ref, bf16[3,512,256]{2,1,0:T(8,128)(2,1)S(1)} %copy-done, bf16[2,128,384]{2,1,0:T(8,128)(2,1)S(1)} %collective-permute-done.halo, bf16[2,3,40,128]{3,2,1,0:T(8,128)(2,1)S(1)} %merge.1.rest_0_, ...), custom_call_target="tpu_custom_call", output_to_operand_aliasing={{}: (7, {})} | custom-call | bytes 8388608 | tf_op jit(solution)/shard_map/late/pallas_call | solution.py:421
Async XLA Ops:
  0.0 1.1 %copy-start = (bf16[3,512,256]{2,1,0:T(8,128)(2,1)S(1)}, bf16[3,512,256]{2,1,0:T(8,128)(2,1)}, u32[]{:S(2)}) copy-start(bf16[3,512,256]{2,1,0:T(8,128)(2,1)} %sky_hbm.5) | copy-start | bytes 2359300
  1.1 0.8 %copy-start.1 = (bf16[3,1,64,64]{3,2,1,0:T(8,128)(2,1)S(1)}, bf16[3,1,64,64]{3,2,1,0:T(8,128)(2,1)}, u32[]{:S(2)}) copy-start(bf16[3,1,64,64]{3,2,1,0:T(8,128)(2,1)} %obs_hbm.1) | copy-start | bytes 73732
  1.9 0.7 %copy-start.2 = (bf16[3,1,625]{2,0,1:T(4,128)(2,1)S(1)}, bf16[3,1,625]{2,0,1:T(4,128)(2,1)}, u32[]{:S(2)}) copy-start(bf16[3,1,625]{2,0,1:T(4,128)(2,1)} %param.7) | copy-start | bytes 11254
  3.4 25.7 %collective-permute-start = (bf16[2,128,384]{2,1,0:T(8,128)(2,1)S(1)}, bf16[2,128,384]{2,1,0:T(8,128)(2,1)S(1)}, u32[]{:S(2)}, u32[]{:S(2)}) collective-permute-start(bf16[2,128,384]{2,1,0:T(8,128)(2,1)S(1)} %get-tuple-element.8), channel_id=1, source_target_pairs={{0,4},{4,0},{8,12},{12,8},{1,5},{5,1},{9,13},{13,9},{2,6},{6,2},{1... | collective-permute-start | bytes 589832 | tf_op jit(solution)/shard_map/ppermute | solution.py:460
  6.5 16.9 %collective-permute-start.6 = (bf16[1,128,384]{2,1,0:T(8,128)(2,1)S(1)}, bf16[1,128,384]{2,1,0:T(8,128)(2,1)S(1)}, u32[]{:S(2)}, u32[]{:S(2)}) collective-permute-start(bf16[1,128,384]{2,1,0:T(8,128)(2,1)S(1)} %get-tuple-element.10), channel_id=1, source_target_pairs={{0,4},{4,0},{8,12},{12,8},{1,5},{5,1},{9,13},{13,9},{2,6},{6,2},{1... | collective-permute-start | bytes 294920 | tf_op jit(solution)/shard_map/ppermute | solution.py:460
  6.6 7.6 %collective-permute-start.1 = (bf16[3,1,64,64]{3,2,1,0:T(8,128)(2,1)S(1)}, bf16[3,1,64,64]{3,2,1,0:T(8,128)(2,1)S(1)}, u32[]{:S(2)}, u32[]{:S(2)}) collective-permute-start(bf16[3,1,64,64]{3,2,1,0:T(8,128)(2,1)S(1)} %copy-done.1), channel_id=1, source_target_pairs={{0,8},{2,10},{4,12},{6,14},{8,0},{10,2},{12,4},{14,6},{1,9},{3,11}... | collective-permute-start | bytes 73736 | tf_op jit(solution)/shard_map/ppermute | solution.py:457
  9.5 4.6 %collective-permute-start.2 = (bf16[3,625]{1,0:T(4,128)(2,1)S(1)}, bf16[3,625]{1,0:T(4,128)(2,1)S(1)}, u32[]{:S(2)}, u32[]{:S(2)}) collective-permute-start(bf16[3,625]{1,0:T(4,128)(2,1)S(1)} %bitcast.2), channel_id=1, source_target_pairs={{0,8},{2,10},{4,12},{6,14},{8,0},{10,2},{12,4},{14,6},{1,9},{3,11}... | collective-permute-start | bytes 11258 | tf_op jit(solution)/shard_map/ppermute | solution.py:457
  14.4 7.6 %collective-permute-start.5 = (bf16[2,3,40,128]{3,2,1,0:T(8,128)(2,1)S(1)}, bf16[2,3,40,128]{3,2,1,0:T(8,128)(2,1)S(1)}, u32[]{:S(2)}, u32[]{:S(2)}) collective-permute-start(bf16[2,3,40,128]{3,2,1,0:T(8,128)(2,1)S(1)} %merge.1.rest_0_), channel_id=1, source_target_pairs={{0,2},{2,0},{4,6},{6,4},{8,10},{10,8},{12,14},{14,12},{1,3},{3,1},... | collective-permute-start | bytes 184328 | tf_op jit(solution)/shard_map/ppermute | solution.py:457
  16.0 6.1 %collective-permute-start.4 = (bf16[2,3,40,128]{3,2,1,0:T(8,128)(2,1)S(1)}, bf16[2,3,40,128]{3,2,1,0:T(8,128)(2,1)S(1)}, u32[]{:S(2)}, u32[]{:S(2)}) collective-permute-start(bf16[2,3,40,128]{3,2,1,0:T(8,128)(2,1)S(1)} %merge.1.rest_0_), channel_id=1, source_target_pairs={{0,6},{2,4},{4,2},{6,0},{8,14},{10,12},{12,10},{14,8},{1,7},{3,5},... | collective-permute-start | bytes 184328 | tf_op jit(solution)/shard_map/ppermute | solution.py:457
  19.2 4.2 %collective-permute-start.3 = (bf16[2,3,40,128]{3,2,1,0:T(8,128)(2,1)S(1)}, bf16[2,3,40,128]{3,2,1,0:T(8,128)(2,1)S(1)}, u32[]{:S(2)}, u32[]{:S(2)}) collective-permute-start(bf16[2,3,40,128]{3,2,1,0:T(8,128)(2,1)S(1)} %merge.1.rest_0_), channel_id=1, source_target_pairs={{0,4},{2,6},{4,0},{6,2},{8,12},{10,14},{12,8},{14,10},{1,5},{3,7},... | collective-permute-start | bytes 184328 | tf_op jit(solution)/shard_map/ppermute | solution.py:457
  19.3 0.7 %copy-start.3 = (s32[3,2,8]{2,1,0:T(2,128)S(1)}, s32[3,2,8]{2,1,0:T(2,128)}, u32[]{:S(2)}) copy-start(s32[3,2,8]{2,1,0:T(2,128)} %offset_ref.1) | copy-start | bytes 580
  19.9 0.7 %copy-start.4 = (s32[3,8]{1,0:T(4,128)S(1)}, s32[3,8]{1,0:T(4,128)}, u32[]{:S(2)}) copy-start(s32[3,8]{1,0:T(4,128)} %anchor_ref.1) | copy-start | bytes 292

commit v3 on v2

v3 whole, which is shorter than its diff:
```python
import functools

import jax
import jax.numpy as jnp
from jax import lax
from jax.experimental import pallas as pl
from jax.experimental.pallas import tpu as pltpu
from jax.sharding import PartitionSpec as P

TILE = 256
PSF = 25
STAMP = 64
HALF = STAMP // 2
WIN = 88
LANES = 128
PAIRS = (PSF + 1) // 2
ROWS = 40
SHARED = 7
ASIDE = 32
WPAD = 96
OWN = TILE // LANES
FOLDED = 3
EDGE = PSF - 1
FOLD = 4
TOGETHER = 2
FIELD = (9, 9, 7)
SMALL_VMEM = 8 << 20
WORK_VMEM = 24 << 20
CUT = 120


def lane_of(shape):
    return lax.broadcasted_iota(jnp.int32, shape, 1)


def row_of(shape):
    return lax.broadcasted_iota(jnp.int32, shape, 0)


def pack_into(blocks_ref, at, obs_ref, psf_ref, rows):
    bands, per_device = obs_ref.shape[:2]
    lines = bands * per_device
    taps = PSF * PSF
    lane = lane_of((lines, LANES))
    turn = (lane_of((LANES, LANES)) + row_of((LANES, LANES))) == LANES - 1
    turn = jnp.where(turn, 1.0, 0.0).astype(jnp.bfloat16)
    tiles = []
    for t in range(pl.cdiv(taps, LANES)):
        tile = psf_ref[:, t * LANES : min((t + 1) * LANES, taps)]
        if tile.shape[1] < LANES:
            tile = jnp.concatenate([tile, jnp.zeros((lines, LANES - tile.shape[1]), tile.dtype)], axis=1)
        tiles.append(jnp.dot(tile, turn, preferred_element_type=jnp.float32))

    def run(first, target, count=PSF):
        t, end = first // LANES, (first + count - 1) // LANES
        value = tiles[t] if end == t else jnp.where(lane < LANES // 2, tiles[t], tiles[end])
        value = pltpu.roll(value, (target + first + 1) % LANES, 1)
        return jnp.where(jnp.bitwise_and(target - lane, LANES - 1) < count, value, 0.0)

    for r in range(8):
        row = jnp.zeros((lines, LANES), jnp.float32)
        for m, aside in ((r, 0), (r + SHARED, ASIDE)):
            if r < SHARED and m < PAIRS:
                row = row + run(2 * PSF * m, aside)
                if 2 * m + 1 < PSF:
                    row = row + run(2 * PSF * m + PSF, aside + STAMP)
        rows[r] = row
    for x in range(per_device):
        for b in range(bands):
            stamp = obs_ref[b, x].astype(jnp.float32)
            both = jnp.concatenate([stamp[:HALF], stamp[HALF:]], axis=1)
            blocks_ref[at + x, b, 0:HALF, :] = both.astype(jnp.bfloat16)
            blocks_ref[at + x, b, HALF:ROWS, :] = rows[:, b * per_device + x, :].astype(jnp.bfloat16)


def prep_kernel(
    sky_hbm, obs_hbm, psf_hbm, anchor_hbm, offset_hbm,
    sky_ref, border_ref, blocks_ref, plan_ref,
    obs, psf, anchor, offset, rows, sems,
):
    bands, rows_total = sky_hbm.shape[:2]
    parity = lax.axis_index("sky") % 2
    copies = []

    def bring(src, dst):
        copies.append(pltpu.make_async_copy(src, dst, sems.at[len(copies)]))

    bring(anchor_hbm, anchor)
    bring(offset_hbm, offset)
    for b in range(bands):
        for t in range(OWN):
            bring(sky_hbm.at[b, :, pl.ds(t * LANES, LANES)], sky_ref.at[b, t])
    bring(psf_hbm, psf)
    bring(obs_hbm, obs)
    for copy in copies:
        copy.start()
    copies[0].wait()
    copies[1].wait()
    list_windows(anchor, offset, plan_ref, bands)
    fold = rows_total // FOLD
    lane = lane_of((fold, LANES))
    base = (1 - parity) * WIN
    for b in range(bands):
        for t in range(OWN):
            copies[2 + b * OWN + t].wait()
        turned = []
        for g in range(FOLD):
            part = sky_ref[b, 1 - parity, g * fold : (g + 1) * fold, :].astype(jnp.float32)
            turned.append(pltpu.roll(part, (base + WIN * g) % LANES, 1))
        for t in range(FOLDED):
            limit = WIN * (t + 1) - LANES * t
            tile = jnp.where(lane < limit, turned[t], turned[t + 1])
            border_ref[b, :, t * LANES : (t + 1) * LANES] = tile.astype(jnp.bfloat16)
    for copy in copies[2 + bands * OWN :]:
        copy.wait()
    pack_into(blocks_ref, 0, obs, psf, rows)


def prep(sky, observed, psf, anchor, offsets, slots):
    bands, rows_total = sky.shape[:2]
    per_device = observed.shape[1]
    hbm = pl.BlockSpec(memory_space=pltpu.HBM)
    vmem = pl.BlockSpec(memory_space=pltpu.VMEM)
    smem = pl.BlockSpec(memory_space=pltpu.SMEM)
    arrays = [pltpu.with_memory_space_constraint(x, pltpu.HBM) for x in (sky, observed, psf, anchor, offsets)]
    return pl.pallas_call(
        prep_kernel,
        out_shape=(
            jax.ShapeDtypeStruct((bands, OWN, rows_total, LANES), jnp.bfloat16),
            jax.ShapeDtypeStruct((bands, rows_total // FOLD, FOLDED * LANES), jnp.bfloat16),
            jax.ShapeDtypeStruct((per_device, bands, ROWS, LANES), jnp.bfloat16),
            jax.ShapeDtypeStruct((2, bands * slots + TOGETHER + 2), jnp.int32),
        ),
        in_specs=[hbm] * 5,
        out_specs=(vmem, vmem, vmem, smem),
        scratch_shapes=[
            pltpu.VMEM(observed.shape, jnp.bfloat16),
            pltpu.VMEM(psf.shape, jnp.bfloat16),
            pltpu.SMEM(anchor.shape, jnp.int32),
            pltpu.SMEM(offsets.shape, jnp.int32),
            pltpu.VMEM((8, bands * per_device, LANES), jnp.float32),
            pltpu.SemaphoreType.DMA((bands * OWN + 4,)),
        ],
        compiler_params=pltpu.CompilerParams(vmem_limit_bytes=SMALL_VMEM),
        cost_estimate=pl.CostEstimate(flops=0, bytes_accessed=1 << 20, transcendentals=0),
        name="prep",
    )(*arrays)


def merge_kernel(own_ref, obs_ref, psf_ref, both_ref, rows):
    both_ref[0:1] = own_ref[...]
    pack_into(both_ref, 1, obs_ref, psf_ref, rows)


def merge(own, observed, psf):
    vmem = pl.BlockSpec(memory_space=pltpu.VMEM)
    return pl.pallas_call(
        merge_kernel,
        out_shape=jax.ShapeDtypeStruct((2 * own.shape[0],) + own.shape[1:], jnp.bfloat16),
        in_specs=[vmem] * 3,
        out_specs=vmem,
        scratch_shapes=[pltpu.VMEM((8, psf.shape[0], LANES), jnp.float32)],
        compiler_params=pltpu.CompilerParams(vmem_limit_bytes=SMALL_VMEM),
        cost_estimate=pl.CostEstimate(flops=0, bytes_accessed=1 << 20, transcendentals=0),
        name="merge",
    )(own, observed, psf)


def list_windows(anchor_ref, offset_ref, plan_ref, bands):
    column = lax.axis_index("sky")
    parity = column % 2
    first = column - parity
    slots = lax.axis_size("sky") * lax.axis_size("exp")
    per_device = anchor_ref.shape[1] // slots
    cap = plan_ref.shape[1]
    begin = parity * TILE

    def code_of(b, n, top, start):
        code = jnp.int32(b << (FIELD[0] + FIELD[1] + FIELD[2]))
        return code + (n << (FIELD[0] + FIELD[1])) + (top << FIELD[1]) + start

    def visit(b, n, counts):
        inner, cross = counts
        for x in range(per_device):
            i = n * per_device + x
            left = offset_ref[b, 1, i]
            here = anchor_ref[b, i] == first
            code = code_of(b, n, offset_ref[b, 0, i], left)
            plan_ref[0, inner] = code - begin
            plan_ref[1, cross] = code - (TILE - LANES)
            start = left - begin
            inner = inner + (here & (start >= 0) & (start <= TILE - WIN)).astype(jnp.int32)
            cross = cross + (here & (left > TILE - WIN) & (left < TILE)).astype(jnp.int32)
        return inner, cross

    counts = (jnp.int32(0), jnp.int32(0))
    for b in range(bands):
        if slots <= 8:
            for n in range(slots):
                counts = visit(b, jnp.int32(n), counts)
        else:
            counts = lax.fori_loop(0, slots, functools.partial(visit, b), counts)
    for k in range(2):
        for extra in range(TOGETHER):
            plan_ref[k, counts[k] + extra] = code_of(bands - 1, jnp.int32(0), jnp.int32(0), jnp.int32(0))
        plan_ref[k, cap - 1] = counts[k]


def unfold(halo, border_ref, b, place, rows_total):
    fold = rows_total // FOLD
    lane = jnp.bitwise_and(lane_of((fold, LANES)) - place, LANES - 1)
    tiles = [border_ref[b, :, t * LANES : (t + 1) * LANES].astype(jnp.float32) for t in range(FOLDED)]
    for g in range(FOLD):
        shift = (place + LANES - WIN * g % LANES) % LANES
        first = WIN * g // LANES
        limit = LANES * (first + 1) - WIN * g
        value = pltpu.roll(tiles[first], shift, 1)
        if limit < WIN:
            value = jnp.where(lane < limit, value, pltpu.roll(tiles[first + 1], shift, 1))
        halo[b, g * fold : (g + 1) * fold, :] = value.astype(jnp.bfloat16)


def work_kernel(late, layout, plan_ref, sky_ref, *rest):
    if late:
        border_ref, near_ref, *rest = rest
    pieces = rest[: len(layout)]
    rest = rest[len(layout) + late :]
    if late:
        out_hbm, halo, *rest = rest
    else:
        out_hbm, near_ref, *rest = rest
    total, blocks, cut, view, banded, wide, rows_a, rows_r, out_sems = rest
    bands, _, rows_total = sky_ref.shape[:3]
    column = lax.axis_index("sky")
    parity = column % 2
    position = column * lax.axis_size("exp") + lax.axis_index("exp")
    mode = int(late)
    mine = list(range(bands))
    for masks, piece in zip(layout, pieces):
        if masks is not None:
            for j, mask in enumerate(masks):
                blocks[jnp.bitwise_xor(position, mask)] = piece[j]
        else:
            blocks = piece
    count = plan_ref[mode, plan_ref.shape[1] - 1]
    rows_r[...] = jnp.zeros(rows_r.shape, jnp.float32)
    for u in range(TOGETHER):
        cut[u, CUT - 8 : CUT, :] = jnp.zeros((8, LANES), jnp.float32)
    for b in mine:
        if late:
            total[b, 0] = near_ref[b]
            unfold(halo, border_ref, b, parity * (LANES - WIN), rows_total)
        else:
            for t in range(OWN):
                total[b, t] = jnp.zeros((rows_total, LANES), jnp.float32)

    lane_w = lane_of((WPAD, LANES))
    gap = row_of((WPAD, LANES)) - lane_w % STAMP
    inside = (gap >= 0) & (gap < PSF) & (row_of((WPAD, LANES)) < WIN)
    lane_c = lane_of((CUT - 8, LANES))
    lane_b = lane_of((WIN, LANES))
    low = lane_of((STAMP, LANES)) < STAMP

    def where_is(job):
        code = plan_ref[mode, job]
        n = jnp.bitwise_and(lax.shift_right_logical(code, FIELD[0] + FIELD[1]), (1 << FIELD[2]) - 1)
        return lax.shift_right_logical(code, FIELD[0] + FIELD[1] + FIELD[2]), n, code

    def fields(job):
        b, n, code = where_is(job)
        top = jnp.bitwise_and(lax.shift_right_logical(code, FIELD[1]), (1 << FIELD[0]) - 1)
        start = jnp.bitwise_and(code, (1 << FIELD[1]) - 1)
        tile = lax.shift_right_logical(start, 7)
        shift = jnp.bitwise_and(start, LANES - 1)
        return b, n, top, tile, shift

    def load_window(job, u):
        b, _, top, tile, shift = fields(job)
        back_shift = jnp.bitwise_and(LANES - shift, LANES - 1)
        base = pl.multiple_of(jnp.minimum(jnp.bitwise_and(top, -16), rows_total - (CUT - 8)), 16)
        span = pl.ds(base, CUT - 8)
        if late:
            own = pltpu.roll(sky_ref[b, 1 - parity, span, :].astype(jnp.float32), back_shift, 1)
            other = pltpu.roll(halo[b, span, :].astype(jnp.float32), back_shift, 1)
            own_from = jnp.where(parity == 0, 0, LANES - shift)
            own_to = jnp.where(parity == 0, LANES - shift, LANES)
            window = jnp.where((lane_c >= own_from) & (lane_c < own_to), own, other)
        else:
            after = jnp.minimum(tile + 1, OWN - 1)
            left = pltpu.roll(sky_ref[b, tile, span, :].astype(jnp.float32), back_shift, 1)
            right = pltpu.roll(sky_ref[b, after, span, :].astype(jnp.float32), back_shift, 1)
            window = jnp.where(lane_c < LANES - shift, left, right)
        cut[u, 0 : CUT - 8, :] = window
        view[u] = cut[u, pl.ds(top - base, WPAD), :].astype(jnp.bfloat16)

    def build(job, u, first, last):
        b, n, _ = where_is(job)
        taps = blocks[n, b, HALF:ROWS, :].astype(jnp.float32)
        for m in range(first, min(last, PAIRS)):
            row = m % SHARED
            spread = jnp.broadcast_to(taps[row : row + 1, :], (WPAD, LANES))
            offset = 0 if m < SHARED else LANES - ASIDE
            turned = pltpu.roll(spread, offset, 1, stride=1, stride_axis=0)
            banded[u, :, m * LANES : (m + 1) * LANES] = jnp.where(inside, turned, 0.0).astype(jnp.bfloat16)

    def forward(u, first, last):
        last = min(last, PAIRS)
        product = jnp.dot(
            view[u, :, :WPAD],
            banded[u, :, first * LANES : last * LANES],
            preferred_element_type=jnp.float32,
        )
        for m in range(first, last):
            wide[u, m] = product[:, (m - first) * LANES : (m - first + 1) * LANES]

    def residual(job, u):
        b, n, _ = where_is(job)
        acc = wide[u, 0, 0:72, :]
        for m in range(1, PAIRS):
            acc = acc + wide[u, m, 2 * m : 2 * m + 72, :]
        rows_a[u] = acc
        model = rows_a[u, 0:STAMP, :] + pltpu.roll(rows_a[u, 1 : STAMP + 1, :], STAMP, 1)
        obs = blocks[n, b, 0:HALF, :].astype(jnp.float32)
        obs = jnp.concatenate([obs, pltpu.roll(obs, STAMP, 1)], axis=0)
        rest = (model - obs).astype(jnp.bfloat16).astype(jnp.float32)
        rest = jnp.where(low, rest, 0.0)
        rows_r[u, EDGE : EDGE + STAMP, :] = rest
        rows_r[u, EDGE + STAMP : EDGE + 72, :] = jnp.zeros((8, LANES), jnp.float32)
        upper = pltpu.roll(rows_r[u, EDGE - 1 : EDGE + 71, :], STAMP, 1)
        rows_r[u, EDGE : EDGE + 72, :] = rows_r[u, EDGE : EDGE + 72, :] + upper

    def backward(u):
        stack = [
            rows_r[u, EDGE - 2 * m : EDGE - 2 * m + WIN, :].astype(jnp.bfloat16) for m in range(PAIRS)
        ]
        back = lax.dot_general(
            jnp.concatenate(stack, axis=1),
            banded[u],
            (((1,), (1,)), ((), ())),
            preferred_element_type=jnp.float32,
        )
        back = back.astype(jnp.bfloat16).astype(jnp.float32)
        return jnp.concatenate([back, jnp.zeros((WIN, LANES - WPAD), jnp.float32)], axis=1)

    def add(job, back):
        b, _, top, tile, shift = fields(job)
        back = pltpu.roll(back, shift, 1)
        live = job < count
        begin = jnp.where(live, shift, LANES)
        end = jnp.where(live, shift, 0)
        here = pl.ds(top, WIN)
        if late:
            own_from = jnp.where(parity == 0, begin, 0)
            own_to = jnp.where(parity == 0, LANES, end)
            total[b, 0, here, :] += jnp.where((lane_b >= own_from) & (lane_b < own_to), back, 0.0)
        else:
            after = jnp.minimum(tile + 1, OWN - 1)
            total[b, tile, here, :] += jnp.where(lane_b >= begin, back, 0.0)
            total[b, after, here, :] += jnp.where(lane_b < end, back, 0.0)

    def out_copy(b):
        side = pl.multiple_of(jnp.where(late, 1 - parity, parity) * LANES, LANES)
        src = total.at[b, 0] if late else total.at[b, parity]
        return pltpu.make_async_copy(src, out_hbm.at[b, :, pl.ds(side, LANES)], out_sems.at[b])

    outs = {b: [out_copy(b)] for b in mine}

    def flush(b, ready):
        @pl.when(ready)
        def _():
            for copy in outs[b]:
                copy.start()

    def step(index, before):
        one = index * 2
        two = one + 1
        now = where_is(one)[0]
        for b in mine[:-1]:
            flush(b, (before <= b) & (now > b))
        load_window(two, 1)
        for c in range(0, PAIRS, 2):
            forward(0, c, c + 2)
            build(two, 1, c, c + 2)
        residual(one, 0)
        for c in range(0, PAIRS, 2):
            forward(1, c, c + 2)
        back_one = backward(0)
        residual(two, 1)
        back_two = backward(1)
        add(one, back_one)
        load_window(one + 2, 0)
        build(one + 2, 0, 0, PAIRS)
        add(two, back_two)
        return now

    load_window(0, 0)
    build(0, 0, 0, PAIRS)
    before = lax.fori_loop(0, lax.div(count + 1, 2), step, jnp.int32(0))
    for b in mine:
        flush(b, before <= b)
    if not late:
        for b in mine:
            near_ref[b] = total[b, 1 - parity]
    for b in mine:
        for copy in outs[b]:
            copy.wait()


def work(late, plan, sky, pieces, layout, slots, border=None, near=None, so_far=None):
    bands, _, rows_total = sky.shape[:3]
    smem = pl.BlockSpec(memory_space=pltpu.SMEM)
    hbm = pl.BlockSpec(memory_space=pltpu.HBM)
    vmem = pl.BlockSpec(memory_space=pltpu.VMEM)
    gathered = (slots, bands, ROWS, LANES) if layout[0] is not None else (1, 1, 8, LANES)
    gradient = jax.ShapeDtypeStruct((bands, rows_total, TILE), jnp.float32)
    first = [border, near] if late else []
    last = [so_far] if late else []
    return pl.pallas_call(
        functools.partial(work_kernel, late, layout),
        out_shape=gradient if late else (gradient, jax.ShapeDtypeStruct((bands, rows_total, LANES), jnp.float32)),
        in_specs=[smem, vmem] + [vmem] * (len(first) + len(pieces)) + [hbm] * len(last),
        out_specs=hbm if late else (hbm, vmem),
        scratch_shapes=([pltpu.VMEM((bands, rows_total, LANES), jnp.bfloat16)] if late else [])
        + [
            pltpu.VMEM((bands, 1 if late else OWN, rows_total, LANES), jnp.float32),
            pltpu.VMEM(gathered, jnp.bfloat16),
            pltpu.VMEM((TOGETHER, CUT, LANES), jnp.float32),
            pltpu.VMEM((TOGETHER, WPAD, LANES), jnp.bfloat16),
            pltpu.VMEM((TOGETHER, WPAD, PAIRS * LANES), jnp.bfloat16),
            pltpu.VMEM((TOGETHER, PAIRS, WPAD, LANES), jnp.float32),
            pltpu.VMEM((TOGETHER, 72, LANES), jnp.float32),
            pltpu.VMEM((TOGETHER, 112, LANES), jnp.float32),
            pltpu.SemaphoreType.DMA((bands,)),
        ],
        compiler_params=pltpu.CompilerParams(vmem_limit_bytes=WORK_VMEM),
        cost_estimate=pl.CostEstimate(flops=0, bytes_accessed=8 << 20, transcendentals=0),
        input_output_aliases={4 + len(pieces): 0} if late else {},
        name="late" if late else "early",
    )(plan, sky, *first, *pieces, *last)


def on_device(sky, observed, psf, anchor, offsets):
    bands = sky.shape[0]
    per_device = observed.shape[1]
    n_sky = lax.axis_size("sky")
    n_exp = lax.axis_size("exp")
    slots = n_sky * n_exp
    both = ("sky", "exp")
    taps = psf.reshape(bands * per_device, psf.shape[-1])
    direct = per_device == 1 and n_sky == 4 and n_exp == 2

    def across(x, mask):
        return lax.ppermute(x, both, [(i, i ^ mask) for i in range(slots)])

    def neighbour(x):
        return lax.ppermute(x, "sky", [(s, s ^ 1) for s in range(n_sky)])

    if direct:
        far_observed = across(observed, 4)
        far_taps = across(taps, 4)
    tiles, border, blocks, plan = prep(sky, observed, taps, anchor, offsets, slots)
    if direct:
        own = merge(blocks, far_observed, far_taps)
        pieces = [own]
        layout = [(0, 4)]
        for mask in (2, 3, 1):
            pieces.append(across(own, mask))
            layout.append((mask, mask ^ 4))
    else:
        position = lax.axis_index("sky") * n_exp + lax.axis_index("exp")
        anchors = anchor.reshape(bands, slots, per_device)
        mine = lax.dynamic_index_in_dim(anchors, position, 1, keepdims=False)
        pair = 2 * jnp.arange(n_sky // 2, dtype=jnp.int32)[:, None, None]
        chosen = jnp.argmax(mine[None] == pair, axis=-1)
        picked = jnp.take_along_axis(blocks[None], chosen[:, None, :, None, None], axis=1)
        send = jnp.broadcast_to(picked, (n_sky // 2, 2 * n_exp, bands, ROWS, LANES))
        send = send.reshape(slots, bands, ROWS, LANES)
        pieces = [lax.all_to_all(send, both, 0, 0, tiled=True)]
        layout = [None]
    halo = neighbour(border)
    so_far, near = work(False, plan, tiles, pieces, layout, slots)
    return work(True, plan, tiles, pieces, layout, slots, halo, near, so_far)


def solution(mesh):
    return jax.shard_map(
        on_device,
        mesh=mesh,
        in_specs=(
            P("band", None, ("group", "sky")),
            P("band", ("group", "sky", "exp"), None, None),
            P("band", ("group", "sky", "exp"), None),
            P("band", "group"),
            P("band", None, "group"),
        ),
        out_specs=P("band", None, ("group", "sky")),
        check_vma=False,
    )
```

time: 33.2 us -> 30.3 us (0.913)
  local copies, waits for them, and re-layouts: 3.98 us -> 0 us
  waiting for transfers between devices: 5.99 us -> 8.75 us
  Pallas kernels: 11.8 us -> 10.3 us
    unnamed x10 -> x0, local copies, waits for them, and re-layouts: 3.98 us -> none
    ppermute x5, waiting for transfers between devices: 5.99 us -> 8.75 us  [across(): return lax.ppermute(x, both, [(i, i ^ mask) for i in range(slots)])]
    pallas_call x4 -> x3, Pallas kernels: 11.6 us -> 10 us  [the longest x2 7.9 us: work(): pl.pallas_call(functools.partial(work_kernel, late, layout), out_shape=gr...]
    ppermute x2 -> x1, starting transfers between devices: 3.2 us -> 3.12 us  [neighbour(): return lax.ppermute(x, 'sky', [(s, s ^ 1) for s in range(n_sky)])]
  transfers between devices with their start and end apart: 7 -> 6, of which waited for: 2 -> 3; matrix products, arithmetic and copies ran while one was open for 0% -> 0% of each run, Pallas kernels for 22% -> 12%
where the time goes in v3:
time: 30.3 us; the launch traced here: 30.1 us
  starting transfers between devices  11 us (36%)
  Pallas kernels  10.3 us (34%)
  waiting for transfers between devices  8.75 us (29%)
    ppermute x5, waiting for transfers between devices, across(): return lax.ppermute(x, both, [(i, i ^ mask) for i in range(slots)])  8.75 us
    ppermute x5, starting transfers between devices, across(): return lax.ppermute(x, both, [(i, i ^ mask) for i in range(slots)])  7.93 us
    pallas_call x2, Pallas kernels, work(): pl.pallas_call(functools.partial(work_kernel, late, layout), out_shape=gr...  7.9 us
    ppermute x1, starting transfers between devices, neighbour(): return lax.ppermute(x, 'sky', [(s, s ^ 1) for s in range(n_sky)])  3.12 us
    pallas_call x1, Pallas kernels, prep(): pl.pallas_call(prep_kernel, out_shape=(jax.ShapeDtypeStruct((bands, OWN,...  2.13 us
  transfers between devices with their start and end apart: 6, of which 3 were waited for; matrix products, arithmetic and copies ran while one was open for 0% of the time, Pallas kernels for 12%

profile of v3, /device:TPU:0, one launch (start us, length us, event | category | flops | bytes accessed | tf_op | source)
XLA Modules:
  0.0 30.1 jit_solution(18276805596987745281)
XLA Ops:
  0.0 2.1 %prep.1 = (bf16[3,2,512,128]{3,2,1,0:T(8,128)(2,1)S(1)}, bf16[3,128,384]{2,1,0:T(8,128)(2,1)S(1)}, bf16[1,3,40,128]{3,2,1,0:T(8,128)(2,1)S(1)}, s32[2,28]{1,0:T(2,128)S(1)}) custom-call(bf16[3,512,256]{2,1,0:T(8,128)(2,1)} %sky_hbm.1, bf16[3,1,64,64]{3,2,1,0:T(8,128)(2,1)} %obs_hbm.1, bf16[3,625]{1,0:T(4,128)(2,1)} %bitcast.1, s32[3,8]{1,0:T(4,128)} %anchor_hbm.1, ...), custom_call_target="tpu_custom_call" | custom-call | bytes 1048576 | tf_op jit(solution)/shard_map/prep/pallas_call | solution.py:126
  2.1 3.1 %collective-permute-start = (bf16[3,128,384]{2,1,0:T(8,128)(2,1)S(1)}, bf16[3,128,384]{2,1,0:T(8,128)(2,1)S(1)}, u32[]{:S(2)}, u32[]{:S(2)}) collective-permute-start(bf16[3,128,384]{2,1,0:T(8,128)(2,1)S(1)} %get-tuple-element.13), channel_id=1, source_target_pairs={{0,4},{4,0},{8,12},{12,8},{1,5},{5,1},{9,13},{13,9},{2,6},{6,2},{1... | collective-permute-start | bytes 884744 | tf_op jit(solution)/shard_map/ppermute | solution.py:456
  5.3 2.6 %collective-permute-start.1 = (bf16[3,1,64,64]{3,2,1,0:T(8,128)(2,1)}, bf16[3,1,64,64]{3,2,1,0:T(8,128)(2,1)S(1)}, u32[]{:S(2)}, u32[]{:S(2)}) collective-permute-start(bf16[3,1,64,64]{3,2,1,0:T(8,128)(2,1)} %obs_hbm.1), channel_id=1, source_target_pairs={{0,8},{2,10},{4,12},{6,14},{8,0},{10,2},{12,4},{14,6},{1,9},{3,11}... | collective-permute-start | bytes 73736 | tf_op jit(solution)/shard_map/ppermute | solution.py:453
  7.8 0.3 %collective-permute-start.2 = (bf16[3,625]{1,0:T(4,128)(2,1)}, bf16[3,625]{1,0:T(4,128)(2,1)S(1)}, u32[]{:S(2)}, u32[]{:S(2)}) collective-permute-start(bf16[3,625]{1,0:T(4,128)(2,1)} %bitcast.2), channel_id=1, source_target_pairs={{0,8},{2,10},{4,12},{6,14},{8,0},{10,2},{12,4},{14,6},{1,9},{3,11}... | collective-permute-start | bytes 11258 | tf_op jit(solution)/shard_map/ppermute | solution.py:453
  8.2 4.6 %collective-permute-done.2.psf_ref = bf16[3,625]{1,0:T(4,128)(2,1)S(1)} collective-permute-done((bf16[3,625]{1,0:T(4,128)(2,1)}, bf16[3,625]{1,0:T(4,128)(2,1)S(1)}, u32[]{:S(2)}, u32[]{:S(2)}) %collective-permute-start.2) | collective-permute-done | bytes 3782 | tf_op jit(solution)/shard_map/ppermute | solution.py:453
  12.7 0.0 collective-permute-done.1.obs_ref
  12.7 0.3 merge.1.rest_0_.rest_2_
  13.0 1.6 %collective-permute-start.5 = (bf16[2,3,40,128]{3,2,1,0:T(8,128)(2,1)S(1)}, bf16[2,3,40,128]{3,2,1,0:T(8,128)(2,1)S(1)}, u32[]{:S(2)}, u32[]{:S(2)}) collective-permute-start(bf16[2,3,40,128]{3,2,1,0:T(8,128)(2,1)S(1)} %merge.1.rest_0_.rest_2_), channel_id=1, source_target_pairs={{0,2},{2,0},{4,6},{6,4},{8,10},{10,8},{12,14},{14,12},{1,3},{3,1},... | collective-permute-start | bytes 184328 | tf_op jit(solution)/shard_map/ppermute | solution.py:453
  14.6 3.4 %collective-permute-start.4 = (bf16[2,3,40,128]{3,2,1,0:T(8,128)(2,1)S(1)}, bf16[2,3,40,128]{3,2,1,0:T(8,128)(2,1)S(1)}, u32[]{:S(2)}, u32[]{:S(2)}) collective-permute-start(bf16[2,3,40,128]{3,2,1,0:T(8,128)(2,1)S(1)} %merge.1.rest_0_.rest_2_), channel_id=1, source_target_pairs={{0,6},{2,4},{4,2},{6,0},{8,14},{10,12},{12,10},{14,8},{1,7},{3,5},... | collective-permute-start | bytes 184328 | tf_op jit(solution)/shard_map/ppermute | solution.py:453
  18.0 0.0 collective-permute-start.3
  18.0 0.0 collective-permute-done.5.rest_3_.rest_5_
  18.0 2.7 %collective-permute-done.4.rest_2_.rest_4_ = bf16[2,3,40,128]{3,2,1,0:T(8,128)(2,1)S(1)} collective-permute-done((bf16[2,3,40,128]{3,2,1,0:T(8,128)(2,1)S(1)}, bf16[2,3,40,128]{3,2,1,0:T(8,128)(2,1)S(1)}, u32[]{:S(2)}, u32[]{:S(2)}) %collective-permute-start.4) | collective-permute-done | bytes 61472 | tf_op jit(solution)/shard_map/ppermute | solution.py:453
  20.7 1.5 %collective-permute-done.3.rest_1_.rest_3_ = bf16[2,3,40,128]{3,2,1,0:T(8,128)(2,1)S(1)} collective-permute-done((bf16[2,3,40,128]{3,2,1,0:T(8,128)(2,1)S(1)}, bf16[2,3,40,128]{3,2,1,0:T(8,128)(2,1)S(1)}, u32[]{:S(2)}, u32[]{:S(2)}) %collective-permute-start.3) | collective-permute-done | bytes 61472 | tf_op jit(solution)/shard_map/ppermute | solution.py:453
  22.2 3.4 %early.1 = (f32[3,512,256]{2,1,0:T(8,128)}, f32[3,512,128]{2,1,0:T(8,128)S(1)}) custom-call(s32[2,28]{1,0:T(2,128)S(1)} %get-tuple-element.11.plan_ref, bf16[3,2,512,128]{3,2,1,0:T(8,128)(2,1)S(1)} %get-tuple-element.12.sky_ref, bf16[2,3,40,128]{3,2,1,0:T(8,128)(2,1)S(1)} %merge.1.rest_0_.rest_2_, ...), custom_call_target="tpu_custom_call" | custom-call | bytes 8388608 | tf_op jit(solution)/shard_map/early/pallas_call | solution.py:418
  25.6 0.0 collective-permute-done.rest_0_
  25.6 4.5 %late.1 = f32[3,512,256]{2,1,0:T(8,128)} custom-call(s32[2,28]{1,0:T(2,128)S(1)} %get-tuple-element.11.plan_ref, bf16[3,2,512,128]{3,2,1,0:T(8,128)(2,1)S(1)} %get-tuple-element.12.sky_ref, bf16[3,128,384]{2,1,0:T(8,128)(2,1)S(1)} %collective-permute-done.rest_0_, f32[3,512,128]{2,1,0:T(8,128)S(1)} %get-tuple-element.15.rest_1_, ...), custom_call_target="tpu_custom_call", output_to_operand_aliasing={{}: (8, {})} | custom-call | bytes 8388608 | tf_op jit(solution)/shard_map/late/pallas_call | solution.py:418
Async XLA Ops:
  2.1 23.4 %collective-permute-start = (bf16[3,128,384]{2,1,0:T(8,128)(2,1)S(1)}, bf16[3,128,384]{2,1,0:T(8,128)(2,1)S(1)}, u32[]{:S(2)}, u32[]{:S(2)}) collective-permute-start(bf16[3,128,384]{2,1,0:T(8,128)(2,1)S(1)} %get-tuple-element.13), channel_id=1, source_target_pairs={{0,4},{4,0},{8,12},{12,8},{1,5},{5,1},{9,13},{13,9},{2,6},{6,2},{1... | collective-permute-start | bytes 884744 | tf_op jit(solution)/shard_map/ppermute | solution.py:456
  5.3 7.5 %collective-permute-start.1 = (bf16[3,1,64,64]{3,2,1,0:T(8,128)(2,1)}, bf16[3,1,64,64]{3,2,1,0:T(8,128)(2,1)S(1)}, u32[]{:S(2)}, u32[]{:S(2)}) collective-permute-start(bf16[3,1,64,64]{3,2,1,0:T(8,128)(2,1)} %obs_hbm.1), channel_id=1, source_target_pairs={{0,8},{2,10},{4,12},{6,14},{8,0},{10,2},{12,4},{14,6},{1,9},{3,11}... | collective-permute-start | bytes 73736 | tf_op jit(solution)/shard_map/ppermute | solution.py:453
  7.8 4.9 %collective-permute-start.2 = (bf16[3,625]{1,0:T(4,128)(2,1)}, bf16[3,625]{1,0:T(4,128)(2,1)S(1)}, u32[]{:S(2)}, u32[]{:S(2)}) collective-permute-start(bf16[3,625]{1,0:T(4,128)(2,1)} %bitcast.2), channel_id=1, source_target_pairs={{0,8},{2,10},{4,12},{6,14},{8,0},{10,2},{12,4},{14,6},{1,9},{3,11}... | collective-permute-start | bytes 11258 | tf_op jit(solution)/shard_map/ppermute | solution.py:453
  13.0 5.0 %collective-permute-start.5 = (bf16[2,3,40,128]{3,2,1,0:T(8,128)(2,1)S(1)}, bf16[2,3,40,128]{3,2,1,0:T(8,128)(2,1)S(1)}, u32[]{:S(2)}, u32[]{:S(2)}) collective-permute-start(bf16[2,3,40,128]{3,2,1,0:T(8,128)(2,1)S(1)} %merge.1.rest_0_.rest_2_), channel_id=1, source_target_pairs={{0,2},{2,0},{4,6},{6,4},{8,10},{10,8},{12,14},{14,12},{1,3},{3,1},... | collective-permute-start | bytes 184328 | tf_op jit(solution)/shard_map/ppermute | solution.py:453
  14.6 6.2 %collective-permute-start.4 = (bf16[2,3,40,128]{3,2,1,0:T(8,128)(2,1)S(1)}, bf16[2,3,40,128]{3,2,1,0:T(8,128)(2,1)S(1)}, u32[]{:S(2)}, u32[]{:S(2)}) collective-permute-start(bf16[2,3,40,128]{3,2,1,0:T(8,128)(2,1)S(1)} %merge.1.rest_0_.rest_2_), channel_id=1, source_target_pairs={{0,6},{2,4},{4,2},{6,0},{8,14},{10,12},{12,10},{14,8},{1,7},{3,5},... | collective-permute-start | bytes 184328 | tf_op jit(solution)/shard_map/ppermute | solution.py:453
  18.0 4.2 %collective-permute-start.3 = (bf16[2,3,40,128]{3,2,1,0:T(8,128)(2,1)S(1)}, bf16[2,3,40,128]{3,2,1,0:T(8,128)(2,1)S(1)}, u32[]{:S(2)}, u32[]{:S(2)}) collective-permute-start(bf16[2,3,40,128]{3,2,1,0:T(8,128)(2,1)S(1)} %merge.1.rest_0_.rest_2_), channel_id=1, source_target_pairs={{0,4},{2,6},{4,0},{6,2},{8,12},{10,14},{12,8},{14,10},{1,5},{3,7},... | collective-permute-start | bytes 184328 | tf_op jit(solution)/shard_map/ppermute | solution.py:453

commit v4 on v3

--- a/solution.py
+++ b/solution.py
@@ -23,6 +23,8 @@
 EDGE = PSF - 1
 FOLD = 4
 TOGETHER = 2
+MODES = 3
+AHEAD = 1
 FIELD = (9, 9, 7)
 SMALL_VMEM = 8 << 20
 WORK_VMEM = 24 << 20
@@ -74,8 +76,8 @@
 
 
 def prep_kernel(
-    sky_hbm, obs_hbm, psf_hbm, anchor_hbm, offset_hbm,
-    sky_ref, border_ref, blocks_ref, plan_ref,
+    distant, sky_hbm, obs_hbm, psf_hbm, anchor_hbm, offset_hbm,
+    sky_ref, first_ref, second_ref, blocks_ref, plan_ref,
     obs, psf, anchor, offset, rows, sems,
 ):
     bands, rows_total = sky_hbm.shape[:2]
@@ -96,7 +98,7 @@
         copy.start()
     copies[0].wait()
     copies[1].wait()
-    list_windows(anchor, offset, plan_ref, bands)
+    list_windows(anchor, offset, plan_ref, bands, distant)
     fold = rows_total // FOLD
     lane = lane_of((fold, LANES))
     base = (1 - parity) * WIN
@@ -110,13 +112,14 @@
         for t in range(FOLDED):
             limit = WIN * (t + 1) - LANES * t
             tile = jnp.where(lane < limit, turned[t], turned[t + 1])
-            border_ref[b, :, t * LANES : (t + 1) * LANES] = tile.astype(jnp.bfloat16)
+            border_ref = first_ref.at[b] if b < AHEAD else second_ref.at[b - AHEAD]
+            border_ref[:, t * LANES : (t + 1) * LANES] = tile.astype(jnp.bfloat16)
     for copy in copies[2 + bands * OWN :]:
         copy.wait()
     pack_into(blocks_ref, 0, obs, psf, rows)
 
 
-def prep(sky, observed, psf, anchor, offsets, slots):
+def prep(sky, observed, psf, anchor, offsets, slots, distant):
     bands, rows_total = sky.shape[:2]
     per_device = observed.shape[1]
     hbm = pl.BlockSpec(memory_space=pltpu.HBM)
@@ -124,15 +127,16 @@
     smem = pl.BlockSpec(memory_space=pltpu.SMEM)
     arrays = [pltpu.with_memory_space_constraint(x, pltpu.HBM) for x in (sky, observed, psf, anchor, offsets)]
     return pl.pallas_call(
-        prep_kernel,
+        functools.partial(prep_kernel, distant),
         out_shape=(
             jax.ShapeDtypeStruct((bands, OWN, rows_total, LANES), jnp.bfloat16),
-            jax.ShapeDtypeStruct((bands, rows_total // FOLD, FOLDED * LANES), jnp.bfloat16),
+            jax.ShapeDtypeStruct((AHEAD, rows_total // FOLD, FOLDED * LANES), jnp.bfloat16),
+            jax.ShapeDtypeStruct((bands - AHEAD, rows_total // FOLD, FOLDED * LANES), jnp.bfloat16),
             jax.ShapeDtypeStruct((per_device, bands, ROWS, LANES), jnp.bfloat16),
-            jax.ShapeDtypeStruct((2, bands * slots + TOGETHER + 2), jnp.int32),
+            jax.ShapeDtypeStruct((MODES, bands * slots + TOGETHER + 2), jnp.int32),
         ),
         in_specs=[hbm] * 5,
-        out_specs=(vmem, vmem, vmem, smem),
+        out_specs=(vmem, vmem, vmem, vmem, smem),
         scratch_shapes=[
             pltpu.VMEM(observed.shape, jnp.bfloat16),
             pltpu.VMEM(psf.shape, jnp.bfloat16),
@@ -166,11 +170,12 @@
     )(own, observed, psf)
 
 
-def list_windows(anchor_ref, offset_ref, plan_ref, bands):
+def list_windows(anchor_ref, offset_ref, plan_ref, bands, distant):
     column = lax.axis_index("sky")
     parity = column % 2
     first = column - parity
     slots = lax.axis_size("sky") * lax.axis_size("exp")
+    position = column * lax.axis_size("exp") + lax.axis_index("exp")
     per_device = anchor_ref.shape[1] // slots
     cap = plan_ref.shape[1]
     begin = parity * TILE
@@ -180,36 +185,43 @@
         return code + (n << (FIELD[0] + FIELD[1])) + (top << FIELD[1]) + start
 
     def visit(b, n, counts):
-        inner, cross = counts
+        near, inner, cross = counts
+        known = jnp.int32(0)
+        if distant:
+            known = (jnp.bitwise_and(n - position, distant - 1) == 0).astype(jnp.int32)
         for x in range(per_device):
             i = n * per_device + x
             left = offset_ref[b, 1, i]
             here = anchor_ref[b, i] == first
             code = code_of(b, n, offset_ref[b, 0, i], left)
-            plan_ref[0, inner] = code - begin
-            plan_ref[1, cross] = code - (TILE - LANES)
+            if distant:
+                plan_ref[0, near] = code - begin
+            plan_ref[1, inner] = code - begin
+            plan_ref[2, cross] = code - (TILE - LANES)
             start = left - begin
-            inner = inner + (here & (start >= 0) & (start <= TILE - WIN)).astype(jnp.int32)
+            inside = (here & (start >= 0) & (start <= TILE - WIN)).astype(jnp.int32)
+            near = near + inside * known
+            inner = inner + inside * (1 - known)
             cross = cross + (here & (left > TILE - WIN) & (left < TILE)).astype(jnp.int32)
-        return inner, cross
-
-    counts = (jnp.int32(0), jnp.int32(0))
+        return near, inner, cross
+
+    counts = (jnp.int32(0),) * MODES
     for b in range(bands):
         if slots <= 8:
             for n in range(slots):
                 counts = visit(b, jnp.int32(n), counts)
         else:
             counts = lax.fori_loop(0, slots, functools.partial(visit, b), counts)
-    for k in range(2):
+    for k in range(MODES):
         for extra in range(TOGETHER):
             plan_ref[k, counts[k] + extra] = code_of(bands - 1, jnp.int32(0), jnp.int32(0), jnp.int32(0))
         plan_ref[k, cap - 1] = counts[k]
 
 
-def unfold(halo, border_ref, b, place, rows_total):
+def unfold(halo, border, b, place, rows_total):
     fold = rows_total // FOLD
     lane = jnp.bitwise_and(lane_of((fold, LANES)) - place, LANES - 1)
-    tiles = [border_ref[b, :, t * LANES : (t + 1) * LANES].astype(jnp.float32) for t in range(FOLDED)]
+    tiles = [border[:, t * LANES : (t + 1) * LANES].astype(jnp.float32) for t in range(FOLDED)]
     for g in range(FOLD):
         shift = (place + LANES - WIN * g % LANES) % LANES
         first = WIN * g // LANES
@@ -220,22 +232,34 @@
         halo[b, g * fold : (g + 1) * fold, :] = value.astype(jnp.bfloat16)
 
 
-def work_kernel(late, layout, plan_ref, sky_ref, *rest):
+def work_kernel(mode, resume, layout, plan_ref, sky_ref, *rest):
+    late = mode == MODES - 1
     if late:
-        border_ref, near_ref, *rest = rest
+        first_ref, second_ref, *rest = rest
+    if resume:
+        sum_ref, *rest = rest
     pieces = rest[: len(layout)]
-    rest = rest[len(layout) + late :]
+    rest = rest[len(layout) :]
     if late:
-        out_hbm, halo, *rest = rest
+        out_hbm, total, halo, out_sems, *rest = rest
     else:
-        out_hbm, near_ref, *rest = rest
-    total, blocks, cut, view, banded, wide, rows_a, rows_r, out_sems = rest
+        total, *rest = rest
+    blocks, cut0, cut1, view, banded0, banded1, wide0, wide1, rows_a, rows_r0, rows_r1 = rest
+    cut, banded, wide, rows_r = (cut0, cut1), (banded0, banded1), (wide0, wide1), (rows_r0, rows_r1)
     bands, _, rows_total = sky_ref.shape[:3]
     column = lax.axis_index("sky")
     parity = column % 2
     position = column * lax.axis_size("exp") + lax.axis_index("exp")
-    mode = int(late)
     mine = list(range(bands))
+
+    def out_copy(src, b, t, at):
+        side = pl.multiple_of(t * LANES, LANES)
+        return pltpu.make_async_copy(src, out_hbm.at[b, :, pl.ds(side, LANES)], out_sems.at[at])
+
+    if late:
+        finished = out_copies = [out_copy(sum_ref.at[b, parity], b, parity, b) for b in mine]
+        for copy in finished:
+            copy.start()
     for masks, piece in zip(layout, pieces):
         if masks is not None:
             for j, mask in enumerate(masks):
@@ -243,16 +267,17 @@
         else:
             blocks = piece
     count = plan_ref[mode, plan_ref.shape[1] - 1]
-    rows_r[...] = jnp.zeros(rows_r.shape, jnp.float32)
     for u in range(TOGETHER):
-        cut[u, CUT - 8 : CUT, :] = jnp.zeros((8, LANES), jnp.float32)
+        rows_r[u][...] = jnp.zeros(rows_r[u].shape, jnp.float32)
+        cut[u][CUT - 8 : CUT, :] = jnp.zeros((8, LANES), jnp.float32)
     for b in mine:
         if late:
-            total[b, 0] = near_ref[b]
-            unfold(halo, border_ref, b, parity * (LANES - WIN), rows_total)
+            total[b, 0] = sum_ref[b, 1 - parity]
+            border = first_ref[b] if b < AHEAD else second_ref[b - AHEAD]
+            unfold(halo, border, b, parity * (LANES - WIN), rows_total)
         else:
             for t in range(OWN):
-                total[b, t] = jnp.zeros((rows_total, LANES), jnp.float32)
+                total[b, t] = sum_ref[b, t] if resume else jnp.zeros((rows_total, LANES), jnp.float32)
 
     lane_w = lane_of((WPAD, LANES))
     gap = row_of((WPAD, LANES)) - lane_w % STAMP
@@ -290,8 +315,8 @@
             left = pltpu.roll(sky_ref[b, tile, span, :].astype(jnp.float32), back_shift, 1)
             right = pltpu.roll(sky_ref[b, after, span, :].astype(jnp.float32), back_shift, 1)
             window = jnp.where(lane_c < LANES - shift, left, right)
-        cut[u, 0 : CUT - 8, :] = window
-        view[u] = cut[u, pl.ds(top - base, WPAD), :].astype(jnp.bfloat16)
+        cut[u][0 : CUT - 8, :] = window
+        view[u] = cut[u][pl.ds(top - base, WPAD), :].astype(jnp.bfloat16)
 
     def build(job, u, first, last):
         b, n, _ = where_is(job)
@@ -301,41 +326,41 @@
             spread = jnp.broadcast_to(taps[row : row + 1, :], (WPAD, LANES))
             offset = 0 if m < SHARED else LANES - ASIDE
             turned = pltpu.roll(spread, offset, 1, stride=1, stride_axis=0)
-            banded[u, :, m * LANES : (m + 1) * LANES] = jnp.where(inside, turned, 0.0).astype(jnp.bfloat16)
+            banded[u][:, m * LANES : (m + 1) * LANES] = jnp.where(inside, turned, 0.0).astype(jnp.bfloat16)
 
     def forward(u, first, last):
         last = min(last, PAIRS)
         product = jnp.dot(
             view[u, :, :WPAD],
-            banded[u, :, first * LANES : last * LANES],
+            banded[u][:, first * LANES : last * LANES],
             preferred_element_type=jnp.float32,
         )
         for m in range(first, last):
-            wide[u, m] = product[:, (m - first) * LANES : (m - first + 1) * LANES]
+            wide[u][m] = product[:, (m - first) * LANES : (m - first + 1) * LANES]
 
     def residual(job, u):
         b, n, _ = where_is(job)
-        acc = wide[u, 0, 0:72, :]
+        acc = wide[u][0, 0:72, :]
         for m in range(1, PAIRS):
-            acc = acc + wide[u, m, 2 * m : 2 * m + 72, :]
+            acc = acc + wide[u][m, 2 * m : 2 * m + 72, :]
         rows_a[u] = acc
         model = rows_a[u, 0:STAMP, :] + pltpu.roll(rows_a[u, 1 : STAMP + 1, :], STAMP, 1)
         obs = blocks[n, b, 0:HALF, :].astype(jnp.float32)
         obs = jnp.concatenate([obs, pltpu.roll(obs, STAMP, 1)], axis=0)
         rest = (model - obs).astype(jnp.bfloat16).astype(jnp.float32)
         rest = jnp.where(low, rest, 0.0)
-        rows_r[u, EDGE : EDGE + STAMP, :] = rest
-        rows_r[u, EDGE + STAMP : EDGE + 72, :] = jnp.zeros((8, LANES), jnp.float32)
-        upper = pltpu.roll(rows_r[u, EDGE - 1 : EDGE + 71, :], STAMP, 1)
-        rows_r[u, EDGE : EDGE + 72, :] = rows_r[u, EDGE : EDGE + 72, :] + upper
+        rows_r[u][EDGE : EDGE + STAMP, :] = rest
+        rows_r[u][EDGE + STAMP : EDGE + 72, :] = jnp.zeros((8, LANES), jnp.float32)
+        upper = pltpu.roll(rows_r[u][EDGE - 1 : EDGE + 71, :], STAMP, 1)
+        rows_r[u][EDGE : EDGE + 72, :] = rows_r[u][EDGE : EDGE + 72, :] + upper
 
     def backward(u):
         stack = [
-            rows_r[u, EDGE - 2 * m : EDGE - 2 * m + WIN, :].astype(jnp.bfloat16) for m in range(PAIRS)
+            rows_r[u][EDGE - 2 * m : EDGE - 2 * m + WIN, :].astype(jnp.bfloat16) for m in range(PAIRS)
         ]
         back = lax.dot_general(
             jnp.concatenate(stack, axis=1),
-            banded[u],
+            banded[u][...],
             (((1,), (1,)), ((), ())),
             preferred_element_type=jnp.float32,
         )
@@ -358,18 +383,16 @@
             total[b, tile, here, :] += jnp.where(lane_b >= begin, back, 0.0)
             total[b, after, here, :] += jnp.where(lane_b < end, back, 0.0)
 
-    def out_copy(b):
-        side = pl.multiple_of(jnp.where(late, 1 - parity, parity) * LANES, LANES)
-        src = total.at[b, 0] if late else total.at[b, parity]
-        return pltpu.make_async_copy(src, out_hbm.at[b, :, pl.ds(side, LANES)], out_sems.at[b])
-
-    outs = {b: [out_copy(b)] for b in mine}
+    if late:
+        closing = [out_copy(total.at[b, 0], b, 1 - parity, bands + b) for b in mine]
+        out_copies = finished + closing
 
     def flush(b, ready):
-        @pl.when(ready)
-        def _():
-            for copy in outs[b]:
-                copy.start()
+        if late:
+
+            @pl.when(ready)
+            def _():
+                closing[b].start()
 
     def step(index, before):
         one = index * 2
@@ -398,45 +421,45 @@
     before = lax.fori_loop(0, lax.div(count + 1, 2), step, jnp.int32(0))
     for b in mine:
         flush(b, before <= b)
-    if not late:
-        for b in mine:
-            near_ref[b] = total[b, 1 - parity]
-    for b in mine:
-        for copy in outs[b]:
+    if late:
+        for copy in out_copies:
             copy.wait()
 
 
-def work(late, plan, sky, pieces, layout, slots, border=None, near=None, so_far=None):
+def work(mode, plan, sky, pieces, layout, slots, so_far=None, borders=()):
+    late = mode == MODES - 1
     bands, _, rows_total = sky.shape[:3]
     smem = pl.BlockSpec(memory_space=pltpu.SMEM)
     hbm = pl.BlockSpec(memory_space=pltpu.HBM)
     vmem = pl.BlockSpec(memory_space=pltpu.VMEM)
     gathered = (slots, bands, ROWS, LANES) if layout[0] is not None else (1, 1, 8, LANES)
-    gradient = jax.ShapeDtypeStruct((bands, rows_total, TILE), jnp.float32)
-    first = [border, near] if late else []
-    last = [so_far] if late else []
+    first = list(borders) + ([] if so_far is None else [so_far])
+    if late:
+        out_shape = jax.ShapeDtypeStruct((bands, rows_total, TILE), jnp.float32)
+        own_scratch = [
+            pltpu.VMEM((bands, 1, rows_total, LANES), jnp.float32),
+            pltpu.VMEM((bands, rows_total, LANES), jnp.bfloat16),
+            pltpu.SemaphoreType.DMA((2 * bands,)),
+        ]
+    else:
+        out_shape = jax.ShapeDtypeStruct((bands, OWN, rows_total, LANES), jnp.float32)
+        own_scratch = []
     return pl.pallas_call(
-        functools.partial(work_kernel, late, layout),
-        out_shape=gradient if late else (gradient, jax.ShapeDtypeStruct((bands, rows_total, LANES), jnp.float32)),
-        in_specs=[smem, vmem] + [vmem] * (len(first) + len(pieces)) + [hbm] * len(last),
-        out_specs=hbm if late else (hbm, vmem),
-        scratch_shapes=([pltpu.VMEM((bands, rows_total, LANES), jnp.bfloat16)] if late else [])
-        + [
-            pltpu.VMEM((bands, 1 if late else OWN, rows_total, LANES), jnp.float32),
-            pltpu.VMEM(gathered, jnp.bfloat16),
-            pltpu.VMEM((TOGETHER, CUT, LANES), jnp.float32),
-            pltpu.VMEM((TOGETHER, WPAD, LANES), jnp.bfloat16),
-            pltpu.VMEM((TOGETHER, WPAD, PAIRS * LANES), jnp.bfloat16),
-            pltpu.VMEM((TOGETHER, PAIRS, WPAD, LANES), jnp.float32),
-            pltpu.VMEM((TOGETHER, 72, LANES), jnp.float32),
-            pltpu.VMEM((TOGETHER, 112, LANES), jnp.float32),
-            pltpu.SemaphoreType.DMA((bands,)),
-        ],
+        functools.partial(work_kernel, mode, so_far is not None, layout),
+        out_shape=out_shape,
+        in_specs=[smem, vmem] + [vmem] * (len(first) + len(pieces)),
+        out_specs=hbm if late else vmem,
+        scratch_shapes=own_scratch
+        + [pltpu.VMEM(gathered, jnp.bfloat16)]
+        + [pltpu.VMEM((CUT, LANES), jnp.float32)] * 2
+        + [pltpu.VMEM((TOGETHER, WPAD, LANES), jnp.bfloat16)]
+        + [pltpu.VMEM((WPAD, PAIRS * LANES), jnp.bfloat16)] * 2
+        + [pltpu.VMEM((PAIRS, WPAD, LANES), jnp.float32)] * 2
+        + [pltpu.VMEM((TOGETHER, 72, LANES), jnp.float32)]
+        + [pltpu.VMEM((112, LANES), jnp.float32)] * 2,
         compiler_params=pltpu.CompilerParams(vmem_limit_bytes=WORK_VMEM),
         cost_estimate=pl.CostEstimate(flops=0, bytes_accessed=8 << 20, transcendentals=0),
-        input_output_aliases={4 + len(pieces): 0} if late else {},
-        name="late" if late else "early",
-    )(plan, sky, *first, *pieces, *last)
+    )(plan, sky, *first, *pieces)
 
 
 def on_device(sky, observed, psf, anchor, offsets):
@@ -458,12 +481,13 @@
     if direct:
         far_observed = across(observed, 4)
         far_taps = across(taps, 4)
-    tiles, border, blocks, plan = prep(sky, observed, taps, anchor, offsets, slots)
+    tiles, ahead, border, blocks, plan = prep(sky, observed, taps, anchor, offsets, slots, slots // 2 if direct else 0)
+    halo_ahead = neighbour(ahead)
     if direct:
         own = merge(blocks, far_observed, far_taps)
         pieces = [own]
         layout = [(0, 4)]
-        for mask in (2, 3, 1):
+        for mask in (3, 2, 1):
             pieces.append(across(own, mask))
             layout.append((mask, mask ^ 4))
     else:
@@ -478,8 +502,11 @@
         pieces = [lax.all_to_all(send, both, 0, 0, tiled=True)]
         layout = [None]
     halo = neighbour(border)
-    so_far, near = work(False, plan, tiles, pieces, layout, slots)
-    return work(True, plan, tiles, pieces, layout, slots, halo, near, so_far)
+    so_far, done = None, 0
+    if direct:
+        so_far, done = work(0, plan, tiles, pieces[:1], layout[:1], slots), 1
+    so_far = work(1, plan, tiles, pieces[done:], layout[done:], slots, so_far)
+    return work(2, plan, tiles, pieces, layout, slots, so_far, (halo_ahead, halo))
 
 
 def solution(mesh):

time: 30.3 us -> 30.6 us (level)
  Pallas kernels: 10.3 us -> 11.3 us
  waiting for transfers between devices: 8.75 us -> 8.22 us
    pallas_call x3 -> x4, Pallas kernels: 10 us -> 11.1 us  [the longest x3 8.99 us: work(): pl.pallas_call(functools.partial(work_kernel, mode, so_far is not None, l...]
    ppermute x5, waiting for transfers between devices: 8.75 us -> 8.21 us  [across(): return lax.ppermute(x, both, [(i, i ^ mask) for i in range(slots)])]
    ppermute x5, starting transfers between devices: 7.93 us -> 7.6 us  [across(): return lax.ppermute(x, both, [(i, i ^ mask) for i in range(slots)])]
    ppermute x1 -> x2, starting transfers between devices: 3.12 us -> 3.2 us  [neighbour(): return lax.ppermute(x, 'sky', [(s, s ^ 1) for s in range(n_sky)])]
  transfers between devices with their start and end apart: 6 -> 7, of which waited for: 3 -> 3; matrix products, arithmetic and copies ran while one was open for 0% -> 0% of each run, Pallas kernels for 12% -> 15%
where the time goes in v4:
time: 30.6 us; the launch traced here: 30.4 us
  Pallas kernels  11.3 us (37%)
  starting transfers between devices  10.8 us (35%)
  waiting for transfers between devices  8.22 us (27%)
    pallas_call x3, Pallas kernels, work(): pl.pallas_call(functools.partial(work_kernel, mode, so_far is not None, l...  8.99 us
    ppermute x5, waiting for transfers between devices, across(): return lax.ppermute(x, both, [(i, i ^ mask) for i in range(slots)])  8.21 us
    ppermute x5, starting transfers between devices, across(): return lax.ppermute(x, both, [(i, i ^ mask) for i in range(slots)])  7.6 us
    ppermute x2, starting transfers between devices, neighbour(): return lax.ppermute(x, 'sky', [(s, s ^ 1) for s in range(n_sky)])  3.2 us
    pallas_call x1, Pallas kernels, prep(): pl.pallas_call(functools.partial(prep_kernel, distant), out_shape=(jax.Sh...  2.1 us
  transfers between devices with their start and end apart: 7, of which 3 were waited for; matrix products, arithmetic and copies ran while one was open for 0% of the time, Pallas kernels for 15%

profile of v4, /device:TPU:0, one launch (start us, length us, event | category | flops | bytes accessed | tf_op | source)
XLA Modules:
  0.0 30.4 jit_solution(1185352291559930281)
XLA Ops:
  0.0 2.1 %prep.1 = (bf16[3,2,512,128]{3,2,1,0:T(8,128)(2,1)S(1)}, bf16[1,128,384]{2,1,0:T(8,128)(2,1)S(1)}, bf16[2,128,384]{2,1,0:T(8,128)(2,1)S(1)}, bf16[1,3,40,128]{3,2,1,0:T(8,128)(2,1)S(1)}, s32[3,28]{1,0:T(4,128)S(1)}) custom-call(bf16[3,512,256]{2,1,0:T(8,128)(2,1)} %sky_hbm.1, bf16[3,1,64,64]{3,2,1,0:T(8,128)(2,1)} %obs_hbm.1, bf16[3,625]{1,0:T(4,128)(2,1)} %bitcast.1, ...), custom_call_target="tpu_custom_call" | custom-call | bytes 1048576 | tf_op jit(solution)/shard_map/prep/pallas_call | solution.py:129
  2.1 3.1 %collective-permute-start.1 = (bf16[2,128,384]{2,1,0:T(8,128)(2,1)S(1)}, bf16[2,128,384]{2,1,0:T(8,128)(2,1)S(1)}, u32[]{:S(2)}, u32[]{:S(2)}) collective-permute-start(bf16[2,128,384]{2,1,0:T(8,128)(2,1)S(1)} %get-tuple-element.13), channel_id=1, source_target_pairs={{0,4},{4,0},{8,12},{12,8},{1,5},{5,1},{9,13},{13,9},{2,6},{6,2},{1... | collective-permute-start | bytes 589832 | tf_op jit(solution)/shard_map/ppermute | solution.py:479
  5.2 0.1 collective-permute-start
  5.3 3.0 %collective-permute-start.2 = (bf16[3,1,64,64]{3,2,1,0:T(8,128)(2,1)}, bf16[3,1,64,64]{3,2,1,0:T(8,128)(2,1)S(1)}, u32[]{:S(2)}, u32[]{:S(2)}) collective-permute-start(bf16[3,1,64,64]{3,2,1,0:T(8,128)(2,1)} %obs_hbm.1), channel_id=1, source_target_pairs={{0,8},{2,10},{4,12},{6,14},{8,0},{10,2},{12,4},{14,6},{1,9},{3,11}... | collective-permute-start | bytes 73736 | tf_op jit(solution)/shard_map/ppermute | solution.py:476
  8.3 0.0 collective-permute-start.3
  8.3 4.8 %collective-permute-done.3.psf_ref = bf16[3,625]{1,0:T(4,128)(2,1)S(1)} collective-permute-done((bf16[3,625]{1,0:T(4,128)(2,1)}, bf16[3,625]{1,0:T(4,128)(2,1)S(1)}, u32[]{:S(2)}, u32[]{:S(2)}) %collective-permute-start.3) | collective-permute-done | bytes 3782 | tf_op jit(solution)/shard_map/ppermute | solution.py:476
  13.1 0.0 collective-permute-done.2.obs_ref
  13.1 0.3 merge.1.rest_0_.rest_3_
  13.4 1.6 %collective-permute-start.6 = (bf16[2,3,40,128]{3,2,1,0:T(8,128)(2,1)S(1)}, bf16[2,3,40,128]{3,2,1,0:T(8,128)(2,1)S(1)}, u32[]{:S(2)}, u32[]{:S(2)}) collective-permute-start(bf16[2,3,40,128]{3,2,1,0:T(8,128)(2,1)S(1)} %merge.1.rest_0_.rest_3_), channel_id=1, source_target_pairs={{0,2},{2,0},{4,6},{6,4},{8,10},{10,8},{12,14},{14,12},{1,3},{3,1},... | collective-permute-start | bytes 184328 | tf_op jit(solution)/shard_map/ppermute | solution.py:476
  14.9 3.1 %collective-permute-start.5 = (bf16[2,3,40,128]{3,2,1,0:T(8,128)(2,1)S(1)}, bf16[2,3,40,128]{3,2,1,0:T(8,128)(2,1)S(1)}, u32[]{:S(2)}, u32[]{:S(2)}) collective-permute-start(bf16[2,3,40,128]{3,2,1,0:T(8,128)(2,1)S(1)} %merge.1.rest_0_.rest_3_), channel_id=1, source_target_pairs={{0,4},{2,6},{4,0},{6,2},{8,12},{10,14},{12,8},{14,10},{1,5},{3,7},... | collective-permute-start | bytes 184328 | tf_op jit(solution)/shard_map/ppermute | solution.py:476
  18.0 0.0 collective-permute-start.4
  18.0 1.7 %shard_map.55.rest_0_ = f32[3,2,512,128]{3,2,1,0:T(8,128)S(1)} custom-call(s32[3,28]{1,0:T(4,128)S(1)} %get-tuple-element.10.plan_ref, bf16[3,2,512,128]{3,2,1,0:T(8,128)(2,1)S(1)} %get-tuple-element.11.sky_ref, bf16[2,3,40,128]{3,2,1,0:T(8,128)(2,1)S(1)} %merge.1.rest_0_.rest_3_), custom_call_target="tpu_custom_call" | custom-call | bytes 8388608 | tf_op jit(solution)/shard_map/pallas_call | solution.py:447
  19.7 0.0 collective-permute-done.6.rest_3_.rest_6_
  19.7 0.5 %collective-permute-done.5.rest_2_.rest_5_ = bf16[2,3,40,128]{3,2,1,0:T(8,128)(2,1)S(1)} collective-permute-done((bf16[2,3,40,128]{3,2,1,0:T(8,128)(2,1)S(1)}, bf16[2,3,40,128]{3,2,1,0:T(8,128)(2,1)S(1)}, u32[]{:S(2)}, u32[]{:S(2)}) %collective-permute-start.5) | collective-permute-done | bytes 61472 | tf_op jit(solution)/shard_map/ppermute | solution.py:476
  20.2 2.9 %collective-permute-done.4.rest_1_.rest_4_ = bf16[2,3,40,128]{3,2,1,0:T(8,128)(2,1)S(1)} collective-permute-done((bf16[2,3,40,128]{3,2,1,0:T(8,128)(2,1)S(1)}, bf16[2,3,40,128]{3,2,1,0:T(8,128)(2,1)S(1)}, u32[]{:S(2)}, u32[]{:S(2)}) %collective-permute-start.4) | collective-permute-done | bytes 61472 | tf_op jit(solution)/shard_map/ppermute | solution.py:476
  23.1 2.7 %shard_map.56.rest_2_ = f32[3,2,512,128]{3,2,1,0:T(8,128)S(1)} custom-call(s32[3,28]{1,0:T(4,128)S(1)} %get-tuple-element.10.plan_ref, bf16[3,2,512,128]{3,2,1,0:T(8,128)(2,1)S(1)} %get-tuple-element.11.sky_ref, f32[3,2,512,128]{3,2,1,0:T(8,128)S(1)} %shard_map.55.rest_0_, bf16[2,3,40,128]{3,2,1,0:T(8,128)(2,1)S(1)} %collective-permute-done.4.rest_1_.rest_4_, ...), custom_call_target="tpu_custom_call" | custom-call | bytes 8388608 | tf_op jit(solution)/shard_map/pallas_call | solution.py:447
  25.8 0.0 collective-permute-done.rest_0_
  25.8 0.0 collective-permute-done.1.rest_1_
  25.8 4.6 %shard_map.57 = f32[3,512,256]{2,1,0:T(8,128)} custom-call(s32[3,28]{1,0:T(4,128)S(1)} %get-tuple-element.10.plan_ref, bf16[3,2,512,128]{3,2,1,0:T(8,128)(2,1)S(1)} %get-tuple-element.11.sky_ref, bf16[1,128,384]{2,1,0:T(8,128)(2,1)S(1)} %collective-permute-done.rest_0_, bf16[2,128,384]{2,1,0:T(8,128)(2,1)S(1)} %collective-permute-done.1.rest_1_, ...), custom_call_target="tpu_custom_call" | custom-call | bytes 8388608 | tf_op jit(solution)/shard_map/pallas_call | solution.py:447
Async XLA Ops:
  2.1 23.7 %collective-permute-start.1 = (bf16[2,128,384]{2,1,0:T(8,128)(2,1)S(1)}, bf16[2,128,384]{2,1,0:T(8,128)(2,1)S(1)}, u32[]{:S(2)}, u32[]{:S(2)}) collective-permute-start(bf16[2,128,384]{2,1,0:T(8,128)(2,1)S(1)} %get-tuple-element.13), channel_id=1, source_target_pairs={{0,4},{4,0},{8,12},{12,8},{1,5},{5,1},{9,13},{13,9},{2,6},{6,2},{1... | collective-permute-start | bytes 589832 | tf_op jit(solution)/shard_map/ppermute | solution.py:479
  5.2 20.6 %collective-permute-start = (bf16[1,128,384]{2,1,0:T(8,128)(2,1)S(1)}, bf16[1,128,384]{2,1,0:T(8,128)(2,1)S(1)}, u32[]{:S(2)}, u32[]{:S(2)}) collective-permute-start(bf16[1,128,384]{2,1,0:T(8,128)(2,1)S(1)} %get-tuple-element.12), channel_id=1, source_target_pairs={{0,4},{4,0},{8,12},{12,8},{1,5},{5,1},{9,13},{13,9},{2,6},{6,2},{1... | collective-permute-start | bytes 294920 | tf_op jit(solution)/shard_map/ppermute | solution.py:479
  5.3 7.8 %collective-permute-start.2 = (bf16[3,1,64,64]{3,2,1,0:T(8,128)(2,1)}, bf16[3,1,64,64]{3,2,1,0:T(8,128)(2,1)S(1)}, u32[]{:S(2)}, u32[]{:S(2)}) collective-permute-start(bf16[3,1,64,64]{3,2,1,0:T(8,128)(2,1)} %obs_hbm.1), channel_id=1, source_target_pairs={{0,8},{2,10},{4,12},{6,14},{8,0},{10,2},{12,4},{14,6},{1,9},{3,11}... | collective-permute-start | bytes 73736 | tf_op jit(solution)/shard_map/ppermute | solution.py:476
  8.3 4.8 %collective-permute-start.3 = (bf16[3,625]{1,0:T(4,128)(2,1)}, bf16[3,625]{1,0:T(4,128)(2,1)S(1)}, u32[]{:S(2)}, u32[]{:S(2)}) collective-permute-start(bf16[3,625]{1,0:T(4,128)(2,1)} %bitcast.2), channel_id=1, source_target_pairs={{0,8},{2,10},{4,12},{6,14},{8,0},{10,2},{12,4},{14,6},{1,9},{3,11}... | collective-permute-start | bytes 11258 | tf_op jit(solution)/shard_map/ppermute | solution.py:476
  13.4 6.3 %collective-permute-start.6 = (bf16[2,3,40,128]{3,2,1,0:T(8,128)(2,1)S(1)}, bf16[2,3,40,128]{3,2,1,0:T(8,128)(2,1)S(1)}, u32[]{:S(2)}, u32[]{:S(2)}) collective-permute-start(bf16[2,3,40,128]{3,2,1,0:T(8,128)(2,1)S(1)} %merge.1.rest_0_.rest_3_), channel_id=1, source_target_pairs={{0,2},{2,0},{4,6},{6,4},{8,10},{10,8},{12,14},{14,12},{1,3},{3,1},... | collective-permute-start | bytes 184328 | tf_op jit(solution)/shard_map/ppermute | solution.py:476
  14.9 5.3 %collective-permute-start.5 = (bf16[2,3,40,128]{3,2,1,0:T(8,128)(2,1)S(1)}, bf16[2,3,40,128]{3,2,1,0:T(8,128)(2,1)S(1)}, u32[]{:S(2)}, u32[]{:S(2)}) collective-permute-start(bf16[2,3,40,128]{3,2,1,0:T(8,128)(2,1)S(1)} %merge.1.rest_0_.rest_3_), channel_id=1, source_target_pairs={{0,4},{2,6},{4,0},{6,2},{8,12},{10,14},{12,8},{14,10},{1,5},{3,7},... | collective-permute-start | bytes 184328 | tf_op jit(solution)/shard_map/ppermute | solution.py:476
  18.0 5.1 %collective-permute-start.4 = (bf16[2,3,40,128]{3,2,1,0:T(8,128)(2,1)S(1)}, bf16[2,3,40,128]{3,2,1,0:T(8,128)(2,1)S(1)}, u32[]{:S(2)}, u32[]{:S(2)}) collective-permute-start(bf16[2,3,40,128]{3,2,1,0:T(8,128)(2,1)S(1)} %merge.1.rest_0_.rest_3_), channel_id=1, source_target_pairs={{0,6},{2,4},{4,2},{6,0},{8,14},{10,12},{12,10},{14,8},{1,7},{3,5},... | collective-permute-start | bytes 184328 | tf_op jit(solution)/shard_map/ppermute | solution.py:476

commit v5 on v4

--- a/solution.py
+++ b/solution.py
@@ -151,23 +151,22 @@
     )(*arrays)
 
 
-def merge_kernel(own_ref, obs_ref, psf_ref, both_ref, rows):
+def merge_kernel(own_ref, far_ref, both_ref):
     both_ref[0:1] = own_ref[...]
-    pack_into(both_ref, 1, obs_ref, psf_ref, rows)
-
-
-def merge(own, observed, psf):
+    both_ref[1:2] = far_ref[...]
+
+
+def merge(own, far):
     vmem = pl.BlockSpec(memory_space=pltpu.VMEM)
     return pl.pallas_call(
         merge_kernel,
         out_shape=jax.ShapeDtypeStruct((2 * own.shape[0],) + own.shape[1:], jnp.bfloat16),
-        in_specs=[vmem] * 3,
+        in_specs=[vmem] * 2,
         out_specs=vmem,
-        scratch_shapes=[pltpu.VMEM((8, psf.shape[0], LANES), jnp.float32)],
         compiler_params=pltpu.CompilerParams(vmem_limit_bytes=SMALL_VMEM),
         cost_estimate=pl.CostEstimate(flops=0, bytes_accessed=1 << 20, transcendentals=0),
         name="merge",
-    )(own, observed, psf)
+    )(own, far)
 
 
 def list_windows(anchor_ref, offset_ref, plan_ref, bands, distant):
@@ -478,13 +477,12 @@
     def neighbour(x):
         return lax.ppermute(x, "sky", [(s, s ^ 1) for s in range(n_sky)])
 
+    tiles, ahead, border, blocks, plan = prep(sky, observed, taps, anchor, offsets, slots, slots // 2 if direct else 0)
     if direct:
-        far_observed = across(observed, 4)
-        far_taps = across(taps, 4)
-    tiles, ahead, border, blocks, plan = prep(sky, observed, taps, anchor, offsets, slots, slots // 2 if direct else 0)
+        far = across(blocks, slots // 2)
     halo_ahead = neighbour(ahead)
     if direct:
-        own = merge(blocks, far_observed, far_taps)
+        own = merge(blocks, far)
         pieces = [own]
         layout = [(0, 4)]
         for mask in (3, 2, 1):

time: 30.6 us -> 29.7 us (0.971)
  waiting for transfers between devices: 8.22 us -> 7.3 us
    ppermute x5 -> x4, waiting for transfers between devices: 8.21 us -> 7.29 us  [across(): return lax.ppermute(x, both, [(i, i ^ mask) for i in range(slots)])]
    ppermute x5 -> x4, starting transfers between devices: 7.6 us -> 7.95 us  [across(): return lax.ppermute(x, both, [(i, i ^ mask) for i in range(slots)])]
  transfers between devices with their start and end apart: 7 -> 6, of which waited for: 3 -> 3; matrix products, arithmetic and copies ran while one was open for 0% -> 0% of each run, Pallas kernels for 15% -> 15%
where the time goes in v5:
time: 29.7 us; the launch traced here: 29.6 us
  Pallas kernels  11.1 us (37%)
  starting transfers between devices  11.1 us (37%)
  waiting for transfers between devices  7.3 us (25%)
    pallas_call x3, Pallas kernels, work(): pl.pallas_call(functools.partial(work_kernel, mode, so_far is not None, l...  8.99 us
    ppermute x4, starting transfers between devices, across(): return lax.ppermute(x, both, [(i, i ^ mask) for i in range(slots)])  7.95 us
    ppermute x4, waiting for transfers between devices, across(): return lax.ppermute(x, both, [(i, i ^ mask) for i in range(slots)])  7.29 us
    ppermute x2, starting transfers between devices, neighbour(): return lax.ppermute(x, 'sky', [(s, s ^ 1) for s in range(n_sky)])  3.2 us
    pallas_call x1, Pallas kernels, prep(): pl.pallas_call(functools.partial(prep_kernel, distant), out_shape=(jax.Sh...  2.1 us
  transfers between devices with their start and end apart: 6, of which 3 were waited for; matrix products, arithmetic and copies ran while one was open for 0% of the time, Pallas kernels for 15%

profile of v5, /device:TPU:0, one launch (start us, length us, event | category | flops | bytes accessed | tf_op | source)
XLA Modules:
  0.0 29.6 jit_solution(43725503117248539)
XLA Ops:
  0.0 2.1 %prep.1 = (bf16[3,2,512,128]{3,2,1,0:T(8,128)(2,1)S(1)}, bf16[1,128,384]{2,1,0:T(8,128)(2,1)S(1)}, bf16[2,128,384]{2,1,0:T(8,128)(2,1)S(1)}, bf16[1,3,40,128]{3,2,1,0:T(8,128)(2,1)S(1)}, s32[3,28]{1,0:T(4,128)S(1)}) custom-call(bf16[3,512,256]{2,1,0:T(8,128)(2,1)} %sky_hbm.1, bf16[3,1,64,64]{3,2,1,0:T(8,128)(2,1)} %obs_hbm.1, bf16[3,625]{1,0:T(4,128)(2,1)} %bitcast.1, ...), custom_call_target="tpu_custom_call" | custom-call | bytes 1048576 | tf_op jit(solution)/shard_map/prep/pallas_call | solution.py:129
  2.1 3.1 %collective-permute-start.1 = (bf16[2,128,384]{2,1,0:T(8,128)(2,1)S(1)}, bf16[2,128,384]{2,1,0:T(8,128)(2,1)S(1)}, u32[]{:S(2)}, u32[]{:S(2)}) collective-permute-start(bf16[2,128,384]{2,1,0:T(8,128)(2,1)S(1)} %get-tuple-element.13), channel_id=1, source_target_pairs={{0,4},{4,0},{8,12},{12,8},{1,5},{5,1},{9,13},{13,9},{2,6},{6,2},{1... | collective-permute-start | bytes 589832 | tf_op jit(solution)/shard_map/ppermute | solution.py:478
  5.2 0.1 collective-permute-start
  5.3 3.0 %collective-permute-start.2 = (bf16[1,3,40,128]{3,2,1,0:T(8,128)(2,1)S(1)}, bf16[1,3,40,128]{3,2,1,0:T(8,128)(2,1)S(1)}, u32[]{:S(2)}, u32[]{:S(2)}) collective-permute-start(bf16[1,3,40,128]{3,2,1,0:T(8,128)(2,1)S(1)} %get-tuple-element.14.own_ref), channel_id=1, source_target_pairs={{0,8},{2,10},{4,12},{6,14},{8,0},{10,2},{12,4},{14,6},{1,9},{3,11}... | collective-permute-start | bytes 92168 | tf_op jit(solution)/shard_map/ppermute | solution.py:475
  8.3 3.9 %collective-permute-done.2.far_ref = bf16[1,3,40,128]{3,2,1,0:T(8,128)(2,1)S(1)} collective-permute-done((bf16[1,3,40,128]{3,2,1,0:T(8,128)(2,1)S(1)}, bf16[1,3,40,128]{3,2,1,0:T(8,128)(2,1)S(1)}, u32[]{:S(2)}, u32[]{:S(2)}) %collective-permute-start.2) | collective-permute-done | bytes 30752 | tf_op jit(solution)/shard_map/ppermute | solution.py:475
  12.2 1.5 %collective-permute-start.5 = (bf16[2,3,40,128]{3,2,1,0:T(8,128)(2,1)S(1)}, bf16[2,3,40,128]{3,2,1,0:T(8,128)(2,1)S(1)}, u32[]{:S(2)}, u32[]{:S(2)}) collective-permute-start(bf16[2,3,40,128]{3,2,1,0:T(8,128)(2,1)S(1)} %merge.1.rest_0_.rest_3_), channel_id=1, source_target_pairs={{0,2},{2,0},{4,6},{6,4},{8,10},{10,8},{12,14},{14,12},{1,3},{3,1},... | collective-permute-start | bytes 184328 | tf_op jit(solution)/shard_map/ppermute | solution.py:475
  13.7 3.5 %collective-permute-start.4 = (bf16[2,3,40,128]{3,2,1,0:T(8,128)(2,1)S(1)}, bf16[2,3,40,128]{3,2,1,0:T(8,128)(2,1)S(1)}, u32[]{:S(2)}, u32[]{:S(2)}) collective-permute-start(bf16[2,3,40,128]{3,2,1,0:T(8,128)(2,1)S(1)} %merge.1.rest_0_.rest_3_), channel_id=1, source_target_pairs={{0,4},{2,6},{4,0},{6,2},{8,12},{10,14},{12,8},{14,10},{1,5},{3,7},... | collective-permute-start | bytes 184328 | tf_op jit(solution)/shard_map/ppermute | solution.py:475
  17.1 0.0 collective-permute-start.3
  17.1 1.7 %shard_map.55.rest_0_ = f32[3,2,512,128]{3,2,1,0:T(8,128)S(1)} custom-call(s32[3,28]{1,0:T(4,128)S(1)} %get-tuple-element.10.plan_ref, bf16[3,2,512,128]{3,2,1,0:T(8,128)(2,1)S(1)} %get-tuple-element.11.sky_ref, bf16[2,3,40,128]{3,2,1,0:T(8,128)(2,1)S(1)} %merge.1.rest_0_.rest_3_), custom_call_target="tpu_custom_call" | custom-call | bytes 8388608 | tf_op jit(solution)/shard_map/pallas_call | solution.py:446
  18.9 0.0 collective-permute-done.5.rest_3_.rest_6_
  18.9 0.5 %collective-permute-done.4.rest_2_.rest_5_ = bf16[2,3,40,128]{3,2,1,0:T(8,128)(2,1)S(1)} collective-permute-done((bf16[2,3,40,128]{3,2,1,0:T(8,128)(2,1)S(1)}, bf16[2,3,40,128]{3,2,1,0:T(8,128)(2,1)S(1)}, u32[]{:S(2)}, u32[]{:S(2)}) %collective-permute-start.4) | collective-permute-done | bytes 61472 | tf_op jit(solution)/shard_map/ppermute | solution.py:475
  19.3 2.9 %collective-permute-done.3.rest_1_.rest_4_ = bf16[2,3,40,128]{3,2,1,0:T(8,128)(2,1)S(1)} collective-permute-done((bf16[2,3,40,128]{3,2,1,0:T(8,128)(2,1)S(1)}, bf16[2,3,40,128]{3,2,1,0:T(8,128)(2,1)S(1)}, u32[]{:S(2)}, u32[]{:S(2)}) %collective-permute-start.3) | collective-permute-done | bytes 61472 | tf_op jit(solution)/shard_map/ppermute | solution.py:475
  22.3 2.7 %shard_map.56.rest_2_ = f32[3,2,512,128]{3,2,1,0:T(8,128)S(1)} custom-call(s32[3,28]{1,0:T(4,128)S(1)} %get-tuple-element.10.plan_ref, bf16[3,2,512,128]{3,2,1,0:T(8,128)(2,1)S(1)} %get-tuple-element.11.sky_ref, f32[3,2,512,128]{3,2,1,0:T(8,128)S(1)} %shard_map.55.rest_0_, bf16[2,3,40,128]{3,2,1,0:T(8,128)(2,1)S(1)} %collective-permute-done.3.rest_1_.rest_4_, ...), custom_call_target="tpu_custom_call" | custom-call | bytes 8388608 | tf_op jit(solution)/shard_map/pallas_call | solution.py:446
  25.0 0.0 collective-permute-done.rest_0_
  25.0 0.0 collective-permute-done.1.rest_1_
  25.0 4.6 %shard_map.57 = f32[3,512,256]{2,1,0:T(8,128)} custom-call(s32[3,28]{1,0:T(4,128)S(1)} %get-tuple-element.10.plan_ref, bf16[3,2,512,128]{3,2,1,0:T(8,128)(2,1)S(1)} %get-tuple-element.11.sky_ref, bf16[1,128,384]{2,1,0:T(8,128)(2,1)S(1)} %collective-permute-done.rest_0_, bf16[2,128,384]{2,1,0:T(8,128)(2,1)S(1)} %collective-permute-done.1.rest_1_, ...), custom_call_target="tpu_custom_call" | custom-call | bytes 8388608 | tf_op jit(solution)/shard_map/pallas_call | solution.py:446
  (1 shorter events, 0.0 us)
Async XLA Ops:
  2.1 22.9 %collective-permute-start.1 = (bf16[2,128,384]{2,1,0:T(8,128)(2,1)S(1)}, bf16[2,128,384]{2,1,0:T(8,128)(2,1)S(1)}, u32[]{:S(2)}, u32[]{:S(2)}) collective-permute-start(bf16[2,128,384]{2,1,0:T(8,128)(2,1)S(1)} %get-tuple-element.13), channel_id=1, source_target_pairs={{0,4},{4,0},{8,12},{12,8},{1,5},{5,1},{9,13},{13,9},{2,6},{6,2},{1... | collective-permute-start | bytes 589832 | tf_op jit(solution)/shard_map/ppermute | solution.py:478
  5.2 19.7 %collective-permute-start = (bf16[1,128,384]{2,1,0:T(8,128)(2,1)S(1)}, bf16[1,128,384]{2,1,0:T(8,128)(2,1)S(1)}, u32[]{:S(2)}, u32[]{:S(2)}) collective-permute-start(bf16[1,128,384]{2,1,0:T(8,128)(2,1)S(1)} %get-tuple-element.12), channel_id=1, source_target_pairs={{0,4},{4,0},{8,12},{12,8},{1,5},{5,1},{9,13},{13,9},{2,6},{6,2},{1... | collective-permute-start | bytes 294920 | tf_op jit(solution)/shard_map/ppermute | solution.py:478
  5.3 6.8 %collective-permute-start.2 = (bf16[1,3,40,128]{3,2,1,0:T(8,128)(2,1)S(1)}, bf16[1,3,40,128]{3,2,1,0:T(8,128)(2,1)S(1)}, u32[]{:S(2)}, u32[]{:S(2)}) collective-permute-start(bf16[1,3,40,128]{3,2,1,0:T(8,128)(2,1)S(1)} %get-tuple-element.14.own_ref), channel_id=1, source_target_pairs={{0,8},{2,10},{4,12},{6,14},{8,0},{10,2},{12,4},{14,6},{1,9},{3,11}... | collective-permute-start | bytes 92168 | tf_op jit(solution)/shard_map/ppermute | solution.py:475
  12.2 6.7 %collective-permute-start.5 = (bf16[2,3,40,128]{3,2,1,0:T(8,128)(2,1)S(1)}, bf16[2,3,40,128]{3,2,1,0:T(8,128)(2,1)S(1)}, u32[]{:S(2)}, u32[]{:S(2)}) collective-permute-start(bf16[2,3,40,128]{3,2,1,0:T(8,128)(2,1)S(1)} %merge.1.rest_0_.rest_3_), channel_id=1, source_target_pairs={{0,2},{2,0},{4,6},{6,4},{8,10},{10,8},{12,14},{14,12},{1,3},{3,1},... | collective-permute-start | bytes 184328 | tf_op jit(solution)/shard_map/ppermute | solution.py:475
  13.7 5.7 %collective-permute-start.4 = (bf16[2,3,40,128]{3,2,1,0:T(8,128)(2,1)S(1)}, bf16[2,3,40,128]{3,2,1,0:T(8,128)(2,1)S(1)}, u32[]{:S(2)}, u32[]{:S(2)}) collective-permute-start(bf16[2,3,40,128]{3,2,1,0:T(8,128)(2,1)S(1)} %merge.1.rest_0_.rest_3_), channel_id=1, source_target_pairs={{0,4},{2,6},{4,0},{6,2},{8,12},{10,14},{12,8},{14,10},{1,5},{3,7},... | collective-permute-start | bytes 184328 | tf_op jit(solution)/shard_map/ppermute | solution.py:475
  17.1 5.1 %collective-permute-start.3 = (bf16[2,3,40,128]{3,2,1,0:T(8,128)(2,1)S(1)}, bf16[2,3,40,128]{3,2,1,0:T(8,128)(2,1)S(1)}, u32[]{:S(2)}, u32[]{:S(2)}) collective-permute-start(bf16[2,3,40,128]{3,2,1,0:T(8,128)(2,1)S(1)} %merge.1.rest_0_.rest_3_), channel_id=1, source_target_pairs={{0,6},{2,4},{4,2},{6,0},{8,14},{10,12},{12,10},{14,8},{1,7},{3,5},... | collective-permute-start | bytes 184328 | tf_op jit(solution)/shard_map/ppermute | solution.py:475
